TPU v7x, 128 devices: a whole 4x4x4 slice. The times are simulated.
128 devices in a mesh: chan: 8 (over x_hi, z), strip: 16 (over x_lo, y, core).
Axes of the slice: x: 4 (x_hi: 2, x_lo: 2; x = x_hi * 2 + x_lo), y: 4, z: 4, core: 2. Of those that a mesh axis runs over, the one named last changes fastest.
Arguments:
- image: float32 [8, 2048, 2048], P('chan', 'strip'), may hold values from 0 to 1
- dual_coeffs: bfloat16 [2, 8, 2048, 2048], P(None, 'chan', 'strip'), may hold values from -4 to 4
- block_ids: int32 [8, 512], P('chan', 'strip'), may hold values from 0 to 63, as said below
- block_counts: int32 [8, 16], P('chan', 'strip'), may hold values from 1 to 32, as said below
- block_weights: bfloat16 [8, 512, 32, 128], P('chan', 'strip'), may hold values from 0.25 to 2
- block_data: bfloat16 [8, 2, 512, 32, 128], P('chan', None, 'strip'), may hold values from -6 to 6
Outputs:
- image_new: float32 [8, 2048, 2048], P('chan', 'strip')
- dual_new: bfloat16 [2, 8, 2048, 2048], P(None, 'chan', 'strip')
Inputs may be any that keep to these rules, and one draw needn't show every extreme that they name: `block_ids`: the 32 ids of one channel and one pencil are distinct. `block_counts`: some channel and pencil has all 32 slots live.
All inputs are finite; a program needn't handle non-finite values.
Results may differ from a plain program's by a relative error of at most 0.0055.
Values sent between devices are 32-bit elements; how exact they have to be, the bound alone decides.
A program may use at most 64 MiB of HBM per device.

v0:
```python
import math

import jax
import jax.numpy as jnp
import numpy as np
from jax import lax
from jax.experimental import pallas as pl
from jax.experimental.pallas import tpu as pltpu
from jax.sharding import PartitionSpec as P

MESH = pl.DeviceIdType.MESH
F32, BF16 = jnp.float32, jnp.bfloat16

PIX = 2048
ROWS = 128
STRIPS = 16
RIM = 8
PAD = ROWS + 2 * RIM
BANKS = 2
QUARTER = ROWS // 4

root_three = math.sqrt(3.0)
sqrt_two = math.sqrt(2.0)
daub_two = [
    (1.0 + root_three) / (4.0 * sqrt_two),
    (3.0 + root_three) / (4.0 * sqrt_two),
    (3.0 - root_three) / (4.0 * sqrt_two),
    (1.0 - root_three) / (4.0 * sqrt_two),
]
daub_four = [
    0.2303778133088964,
    0.7148465705529155,
    0.6308807679298587,
    -0.0279837694168599,
    -0.1870348117190931,
    0.0308413818355607,
    0.0328830116668852,
    -0.010597401785069,
]
bank_filters = [daub_two, daub_four]
sigma_dual = 0.5
tau_primal = 0.3
shrink_level = 0.5


def bank_matrix(taps, out_at, out_count, in_at, in_count):
    count = len(taps)
    high = [(-1) ** k * taps[count - 1 - k] for k in range(count)]
    offset = count // 2 - 1
    matrix = np.zeros((out_count, in_count), np.float64)
    for i in range(out_count):
        m = out_at + i
        even = m - m % 2
        for k in range(count):
            n = even + k - offset - in_at
            if 0 <= n < in_count:
                matrix[i, n] = (taps if m % 2 == 0 else high)[k]
    return matrix


def make_constants():
    two_pi = 2.0 * math.pi
    tables = []
    for parity in range(2):
        tile, part, k = np.meshgrid(np.arange(8), np.arange(2), np.arange(64), indexing="ij")
        freq = 128 * tile + 2 * k + parity
        phase = part * (math.pi / 2)
        if parity == 0:
            freq[0, 1, 0] = PIX // 2
            phase = phase.copy()
            phase[0, 1, 0] = 0.0
        freq, phase = freq.reshape(-1), phase.reshape(-1)
        coarse = two_pi * (32 * np.arange(32)[:, None] * freq[None, :] % PIX) / PIX
        fine = two_pi * (np.arange(32)[:, None] * freq[None, :] % PIX) / PIX + phase[None, :]
        tables += [np.cos(coarse), np.sin(coarse), np.cos(fine) / 32.0, np.sin(fine) / 32.0]
    tables = np.stack(tables).astype(np.float32)
    grid = two_pi * (np.arange(512)[:, None] * np.arange(512)[None, :] % 512) / 512
    fourier = np.concatenate([np.cos(grid), np.sin(grid)], axis=1) / 64.0
    twiddle = np.zeros((512, 128), np.float32)
    for u in (1, 2, 3):
        angle = two_pi * (np.arange(512) * u) / PIX
        twiddle[:, 2 * u - 2] = np.cos(angle)
        twiddle[:, 2 * u - 1] = np.sin(angle)
    ana_cols = np.concatenate(
        [bank_matrix(t, 128, 128, 0, 384).T for t in bank_filters], axis=1
    )
    ana_rows = np.stack([sigma_dual * bank_matrix(t, RIM, ROWS, 0, PAD) for t in bank_filters])
    syn_rows = np.stack([bank_matrix(t, 0, PAD, RIM, ROWS).T for t in bank_filters])
    syn_cols = np.concatenate([bank_matrix(t, 0, 384, 128, 128) for t in bank_filters], axis=0)
    as_bf16 = lambda a: np.asarray(a, np.float32).astype(BF16)
    return (
        tables,
        as_bf16(fourier),
        twiddle,
        as_bf16(ana_cols),
        as_bf16(ana_rows),
        as_bf16(syn_rows),
        as_bf16(syn_cols),
    )


def dot(a, b):
    return jnp.dot(a, b, preferred_element_type=F32)


def swap_halves(values):
    tiles = [
        pltpu.roll(values[:, 128 * t : 128 * t + 128], 64, 1)
        for t in range(values.shape[1] // 128)
    ]
    return jnp.concatenate(tiles, axis=1) if len(tiles) > 1 else tiles[0]


def lanes(shape):
    return lax.broadcasted_iota(jnp.int32, shape, len(shape) - 1)


def loop(count, body):
    def step(i, carry):
        body(i)
        return carry

    lax.fori_loop(0, count, step, 0)


def at(i, width):
    return pl.ds(pl.multiple_of(i * width, width), width)


def kernel(
    image_hbm, dual_hbm, ids_ref, counts_ref, weights_hbm, data_hbm,
    tables_hbm, fourier_hbm, twiddle_hbm, ana_cols_hbm, ana_rows_hbm, syn_rows_hbm, syn_cols_hbm,
    image_out, dual_out,
    xpad, xwide, dual, weights, data, tables, fourier, twiddle, ana_cols, ana_rows, syn_rows, syn_cols,
    basis, folded, ysend, yrecv, hsend, hrecv, coeffs, trial, squares, near, far, quarter_sum, other_sum,
    factor, combined, edge_send, edge_recv, synth_wide, adjoint, wd_flat, wd_dense, forward, backward,
    packed, image_new, dual_new,
    local_sem, y_s, y_r, h_s, h_r, halo_s, halo_r, edge_s, edge_r, far_s, far_r, near_s, near_r,
    x_s, x_r, ga_s, ga_r, gb_s, gb_r, out_sem,
):
    me = lax.axis_index("strip")
    chan = lax.axis_index("chan")
    z = chan % 4
    x_hi = chan // 4
    zp, zm, zf = (z + 1) % 4, (z + 3) % 4, (z + 2) % 4
    up = {"chan": x_hi * 4 + zp}
    down = {"chan": x_hi * 4 + zm}
    across = {"chan": (1 - x_hi) * 4 + z}
    before, after = {"strip": (me + 15) % STRIPS}, {"strip": (me + 1) % STRIPS}
    sign = jnp.where(me < 8, 1, -1)

    loads = [
        pltpu.make_async_copy(src, dst, local_sem.at[i])
        for i, (src, dst) in enumerate(
            [
                (image_hbm, xpad.at[RIM : RIM + ROWS]),
                (tables_hbm, tables),
                (ana_cols_hbm, ana_cols),
                (ana_rows_hbm, ana_rows),
                (dual_hbm, dual),
                (weights_hbm, weights),
                (data_hbm, data),
                (fourier_hbm, fourier),
                (twiddle_hbm, twiddle),
                (syn_rows_hbm, syn_rows),
                (syn_cols_hbm, syn_cols),
            ]
        )
    ]
    for load in loads:
        load.start()

    barrier = pltpu.get_barrier_semaphore()
    for k in range(1, STRIPS):
        pl.semaphore_signal(
            barrier, inc=1, device_id={"strip": (me + k) % STRIPS}, device_id_type=MESH
        )
    for peer in (up, down, across):
        pl.semaphore_signal(barrier, inc=1, device_id=peer, device_id_type=MESH)
    pl.semaphore_wait(barrier, STRIPS + 2)

    def remote(src, dst, send, recv, peer):
        return pltpu.make_async_remote_copy(
            src_ref=src, dst_ref=dst, send_sem=send, recv_sem=recv, device_id=peer, device_id_type=MESH
        )

    halos = [
        remote(xpad.at[RIM : 2 * RIM], xpad.at[RIM + ROWS : PAD], halo_s.at[0], halo_r.at[0], before),
        remote(xpad.at[ROWS : RIM + ROWS], xpad.at[0:RIM], halo_s.at[1], halo_r.at[1], after),
    ]
    loads[0].wait()
    for copy in halos:
        copy.start()

    loads[1].wait()
    for parity in range(2):
        def make_basis(i, parity=parity):
            coarse_cos = tables[4 * parity, pl.ds(i, 1), :]
            coarse_sin = tables[4 * parity + 1, pl.ds(i, 1), :]
            block = coarse_cos * tables[4 * parity + 2] - coarse_sin * tables[4 * parity + 3]
            basis[parity, at(i, 32), :] = block.astype(BF16)

        loop(32, make_basis)
    left, right = xpad[RIM : RIM + ROWS, 0:1024], xpad[RIM : RIM + ROWS, 1024:2048]
    folded[0] = (left + right).astype(BF16)
    folded[1] = (left - right).astype(BF16)
    for parity in range(2):
        for pair in range(4):
            tiles = dot(folded[parity], basis[parity, :, 256 * pair : 256 * pair + 256])
            for half in range(2):
                tile = tiles[:, 128 * half : 128 * half + 128]
                p = 2 * pair + half
                ysend[p, :, 128 * parity : 128 * parity + 128] = tile
                if parity == 1:
                    ysend[15 - p, :, 128:256] = tile
    lane = lanes((ROWS, 128))
    edge_lane = (lane == 0) | (lane == 64)
    first = ysend[0, :, 0:128]
    for p in range(7):
        ysend[15 - p, :, 0:128] = jnp.where(edge_lane, ysend[p + 1, :, 0:128], ysend[p, :, 0:128])
    ysend[8, :, 0:128] = jnp.where(
        lane == 0, pltpu.roll(first, 64, 1), jnp.where(lane == 64, 0.0, ysend[7, :, 0:128])
    )
    ysend[0, :, 0:128] = jnp.where(lane == 64, 0.0, first)

    def y_copy(k):
        q = (me + k) % STRIPS
        return remote(ysend.at[q], yrecv.at[at(me, ROWS)], y_s.at[k], y_r.at[k], {"strip": q})

    for k in range(1, STRIPS):
        y_copy(k).start()
    yrecv[at(me, ROWS), :] = ysend[me]

    for copy in halos:
        copy.wait_recv()
    for i in (2, 3, 4):
        loads[i].wait()
    xwide[:, 0:128] = jnp.zeros((PAD, 128), BF16)
    xwide[:, 128 + PIX : 256 + PIX] = jnp.zeros((PAD, 128), BF16)
    row = lax.broadcasted_iota(jnp.int32, (PAD, PIX), 0)
    outside = ((row < RIM) & (me == 0)) | ((row >= RIM + ROWS) & (me == STRIPS - 1))
    xwide[:, 128 : 128 + PIX] = jnp.where(outside, 0.0, xpad[...]).astype(BF16)

    def analyse_columns(t):
        start = pl.multiple_of(t * 128, 128)
        both = dot(xwide[:, pl.ds(start, 384)], ana_cols[...]).astype(BF16)
        coeffs[0, :, pl.ds(start, 128)] = both[:, 0:128]
        coeffs[1, :, pl.ds(start, 128)] = both[:, 128:256]

    loop(16, analyse_columns)

    def far_copies(bank):
        return [
            remote(
                squares.at[bank, pl.ds(pl.multiple_of(zf * QUARTER, QUARTER), 16)],
                far.at[bank, 0], far_s.at[2 * bank], far_r.at[2 * bank], up,
            ),
            remote(
                squares.at[bank, pl.ds(pl.multiple_of(zf * QUARTER + 16, 16), 16)],
                far.at[bank, 1], far_s.at[2 * bank + 1], far_r.at[2 * bank + 1], down,
            ),
        ]

    def near_copies(bank):
        return [
            remote(
                squares.at[bank, at(zp, QUARTER)], near.at[bank, 0],
                near_s.at[2 * bank], near_r.at[2 * bank], up,
            ),
            remote(
                squares.at[bank, at(zm, QUARTER)], near.at[bank, 1],
                near_s.at[2 * bank + 1], near_r.at[2 * bank + 1], down,
            ),
        ]

    def x_copy(bank):
        return remote(quarter_sum.at[bank], other_sum.at[bank], x_s.at[bank], x_r.at[bank], across)

    def gather_near(bank):
        mine = factor.at[bank, at(z, QUARTER)]
        return [
            remote(mine, mine, ga_s.at[2 * bank], ga_r.at[2 * bank], up),
            remote(mine, mine, ga_s.at[2 * bank + 1], ga_r.at[2 * bank + 1], down),
        ]

    def gather_far(bank):
        low = factor.at[bank, pl.ds(pl.multiple_of(zm * QUARTER, QUARTER), 16)]
        high = factor.at[bank, pl.ds(pl.multiple_of(zp * QUARTER + 16, 16), 16)]
        return [
            remote(low, low, gb_s.at[2 * bank], gb_r.at[2 * bank], up),
            remote(high, high, gb_s.at[2 * bank + 1], gb_r.at[2 * bank + 1], down),
        ]

    for bank in range(BANKS):
        def analyse_rows(t, bank=bank):
            cols = at(t, 512)
            values = dual[bank, :, cols].astype(F32) + dot(ana_rows[bank], coeffs[bank, :, cols])
            trial[bank, :, cols] = values
            squares[bank, :, cols] = values * values

        loop(4, analyse_rows)
        for copy in far_copies(bank):
            copy.start()

    for i in (5, 6, 7, 8):
        loads[i].wait()
    lane256 = lanes((128, 256))
    column = 2 * (lane256 % 64) + lane256 // 128
    column = jnp.where(me < 8, column, (128 - column) % 128)
    hit = lax.broadcasted_iota(jnp.int32, (128, 256), 0) == column
    imag_lane = (lane256 // 64) % 2 == 1
    pick_both = jnp.where(hit, 1.0, 0.0).astype(BF16)
    pick_real = jnp.where(hit & ~imag_lane, 1.0, 0.0).astype(BF16)
    pick_imag = (jnp.where(hit & imag_lane, 1.0, 0.0) * sign.astype(F32)).astype(BF16)

    def pick_columns(i):
        rows = at(i, 256)
        blocks = at(i, 8)
        flat = (
            dot(weights[blocks].reshape(256, 128), pick_both),
            dot(data[0, blocks].reshape(256, 128), pick_real)
            + dot(data[1, blocks].reshape(256, 128), pick_imag),
        )
        for kind in range(2):
            for half in range(2):
                wd_flat[2 * kind + half, rows, :] = flat[kind][:, 128 * half : 128 * half + 128]

    loop(4, pick_columns)
    slot = lanes((8, 32))
    live_ids = jnp.where(slot < counts_ref[...], ids_ref[...], -1).astype(F32).astype(BF16)
    spread = jnp.where(
        lanes((32, 256)) // 8 == lax.broadcasted_iota(jnp.int32, (32, 256), 0), 1.0, 0.0
    ).astype(BF16)
    slot_ids = dot(live_ids, spread)[0:1, :].astype(jnp.int32)
    place_row = lax.broadcasted_iota(jnp.int32, (512, 256), 0)
    place_col = lanes((512, 256))
    place = jnp.where(
        (slot_ids == place_row // 8) & (place_row % 8 == place_col % 8), 1.0, 0.0
    ).astype(BF16)
    for kind in range(2):
        for u in range(4):
            picked = jnp.concatenate(
                [
                    wd_flat[2 * kind, pl.ds(u, 256, stride=4), :],
                    wd_flat[2 * kind + 1, pl.ds(u, 256, stride=4), :],
                ],
                axis=1,
            ).astype(BF16)
            wd_dense[kind, u] = dot(place, picked).astype(BF16)

    for bank in range(BANKS):
        for copy in far_copies(bank):
            copy.wait_recv()
        low = pl.ds(pl.multiple_of(zp * QUARTER, QUARTER), 16)
        high = pl.ds(pl.multiple_of(zm * QUARTER + 16, 16), 16)
        squares[bank, low, :] = squares[bank, low, :] + far[bank, 0]
        squares[bank, high, :] = squares[bank, high, :] + far[bank, 1]
        for copy in near_copies(bank):
            copy.start()
    for bank in range(BANKS):
        for copy in near_copies(bank):
            copy.wait_recv()
        quarter_sum[bank] = squares[bank, at(z, QUARTER), :] + near[bank, 0] + near[bank, 1]
        x_copy(bank).start()

    lane_sign = jnp.where((lanes((1, 256)) // 64) % 2 == 0, -sign, sign).astype(F32)
    for k in range(1, STRIPS):
        y_copy(k).wait_recv()

    def fold_rows(i):
        rows = at(i, 64)
        low = pl.ds(pl.multiple_of(512 + i * 64, 64), 64)
        y0, y1, y2, y3 = (
            yrecv[pl.ds(pl.multiple_of(512 * j + i * 64, 64), 64), :] for j in range(4)
        )
        tw = twiddle[rows, :]
        c1, s1, c2, s2, c3, s3 = (tw[:, j : j + 1] for j in range(6))
        sum_a, sum_b, dif_a, dif_b = y0 + y2, y1 + y3, y0 - y2, y1 - y3
        forward[0, rows, 0:256] = (sum_a + sum_b).astype(BF16)
        alt = sum_a - sum_b
        parts = (
            (c1 * dif_a - s1 * dif_b, -c1 * dif_b - s1 * dif_a),
            (c2 * alt, -s2 * alt),
            (c3 * dif_a + s3 * dif_b, c3 * dif_b - s3 * dif_a),
        )
        for u, (real, imag) in enumerate(parts, 1):
            real, imag = real.astype(BF16), imag.astype(BF16)
            forward[u, rows, 0:256] = real
            forward[u, low, 0:256] = imag
            forward[u, rows, 256:512] = imag
            forward[u, low, 256:512] = -real

    loop(8, fold_rows)

    for u in range(4):
        def weigh(m, u=u):
            rows = at(m, 128)
            low = pl.ds(pl.multiple_of(512 + m * 128, 128), 128)
            if u == 0:
                real = dot(fourier[rows, 0:512], forward[0, 0:512, 0:256])
                imag = -dot(fourier[rows, 512:1024], forward[0, 0:512, 0:256])
            else:
                both = dot(fourier[rows, :], forward[u])
                real, imag = both[:, 0:256], both[:, 256:512]
            spectrum = real + lane_sign * swap_halves(imag)
            weight = wd_dense[0, u, rows, :].astype(F32)
            residual = weight * (weight * spectrum - wd_dense[1, u, rows, :].astype(F32))
            turned = (lane_sign * swap_halves(residual)).astype(BF16)
            residual = residual.astype(BF16)
            backward[u, rows, 0:256] = residual
            backward[u, low, 0:256] = turned
            if u > 0:
                backward[u, rows, 256:512] = -turned
                backward[u, low, 256:512] = residual

        loop(4, weigh)

    def unfold_rows(m):
        rows = at(m, 128)
        left_side = fourier[rows, :]
        tw = twiddle[rows, :]
        c1, s1, c2, s2, c3, s3 = (tw[:, j : j + 1] for j in range(6))
        k0 = dot(left_side, backward[0, :, 0:256])
        k1, k2, k3 = (dot(left_side, backward[u]) for u in (1, 2, 3))
        r1 = c1 * k1[:, 0:256] - s1 * k1[:, 256:512]
        i1 = c1 * k1[:, 256:512] + s1 * k1[:, 0:256]
        r2 = c2 * k2[:, 0:256] - s2 * k2[:, 256:512]
        r3 = c3 * k3[:, 0:256] - s3 * k3[:, 256:512]
        i3 = c3 * k3[:, 256:512] + s3 * k3[:, 0:256]
        plus, minus, real, imag = k0 + r2, k0 - r2, r1 + r3, i3 - i1
        for j, value in enumerate((plus + real, minus + imag, plus - real, minus - imag)):
            hsend[pl.ds(pl.multiple_of(512 * j + m * 128, 128), 128), :] = value

    loop(4, unfold_rows)

    def h_copy(k):
        q = (me + k) % STRIPS
        return remote(hsend.at[at(q, ROWS)], hrecv.at[me], h_s.at[k], h_r.at[k], {"strip": q})

    for k in range(1, STRIPS):
        h_copy(k).start()
    hrecv[me] = hsend[at(me, ROWS), :]

    bound = shrink_level * math.sqrt(8.0)
    for bank in range(BANKS):
        x_copy(bank).wait_recv()
        total = quarter_sum[bank] + other_sum[bank]
        factor[bank, at(z, QUARTER), :] = bound / jnp.maximum(jnp.sqrt(total), bound)
        for copy in gather_near(bank):
            copy.start()
    for bank in range(BANKS):
        for copy in gather_near(bank):
            copy.wait_recv()
        for copy in gather_far(bank):
            copy.start()

    dual_outs = []
    for bank in range(BANKS):
        for copy in gather_far(bank):
            copy.wait_recv()

        def shrink(i, bank=bank):
            rows = at(i, 16)
            fresh = (trial[bank, rows, :] * factor[bank, rows, :]).astype(BF16)
            dual_new[bank, rows, :] = fresh
            inner = pl.ds(pl.multiple_of(RIM + i * 16, 8), 16)
            combined[bank, inner, :] = 2.0 * fresh.astype(F32) - dual[bank, rows, :].astype(F32)

        loop(8, shrink)
        edge_send[bank, 0] = combined[bank, RIM : 2 * RIM]
        edge_send[bank, 1] = combined[bank, ROWS : RIM + ROWS]
        for copy in edge_copies(remote, bank, edge_send, edge_recv, edge_s, edge_r, before, after):
            copy.start()
    dual_copy = pltpu.make_async_copy(dual_new, dual_out, out_sem.at[0])
    dual_copy.start()

    for bank in range(BANKS):
        for copy in edge_copies(remote, bank, edge_send, edge_recv, edge_s, edge_r, before, after):
            copy.wait_recv()
        combined[bank, RIM + ROWS : PAD] = jnp.where(me == STRIPS - 1, 0.0, edge_recv[bank, 0])
        combined[bank, 0:RIM] = jnp.where(me == 0, 0.0, edge_recv[bank, 1])
    for i in (9, 10):
        loads[i].wait()
    for bank in range(BANKS):
        synth_wide[bank, :, 0:128] = jnp.zeros((ROWS, 128), BF16)
        synth_wide[bank, :, 128 + PIX : 256 + PIX] = jnp.zeros((ROWS, 128), BF16)

        def synthesise_rows(t, bank=bank):
            values = dot(syn_rows[bank], combined[bank, :, at(t, 512)].astype(BF16))
            synth_wide[bank, :, pl.ds(pl.multiple_of(128 + t * 512, 128), 512)] = values.astype(BF16)

        loop(4, synthesise_rows)

    def synthesise_columns(t):
        start = pl.multiple_of(t * 128, 128)
        window = pl.ds(start, 384)
        adjoint[:, pl.ds(start, 128)] = dot(synth_wide[0, :, window], syn_cols[0:384]) + dot(
            synth_wide[1, :, window], syn_cols[384:768]
        )

    loop(16, synthesise_columns)

    for k in range(1, STRIPS):
        h_copy(k).wait_recv()
    for p in range(8):
        own = hrecv[p, :, 0:128]
        if p == 0:
            even = jnp.where(
                lane == 0, own,
                jnp.where(lane == 64, pltpu.roll(hrecv[8, :, 0:128], 64, 1), own + hrecv[15, :, 0:128]),
            )
        else:
            even = own + jnp.where(edge_lane, hrecv[16 - p, :, 0:128], hrecv[15 - p, :, 0:128])
        odd = hrecv[p, :, 128:256] + hrecv[15 - p, :, 128:256]
        packed[0, :, 128 * p : 128 * p + 128] = even.astype(BF16)
        packed[1, :, 128 * p : 128 * p + 128] = odd.astype(BF16)

    def finish(i):
        cols = at(i, 256)
        turn = (((1,), (1,)), ((), ()))
        even, odd = (
            lax.dot_general(packed[j], basis[j, cols, :], turn, preferred_element_type=F32)
            for j in range(2)
        )
        for gradient, where in (
            (even + odd, cols),
            (even - odd, pl.ds(pl.multiple_of(1024 + i * 256, 256), 256)),
        ):
            image_new[:, where] = jnp.maximum(
                xpad[RIM : RIM + ROWS, where] - tau_primal * (gradient + adjoint[:, where]), 0.0
            )

    loop(4, finish)
    image_copy = pltpu.make_async_copy(image_new, image_out, out_sem.at[1])
    image_copy.start()

    for copy in halos:
        copy.wait_send()
    for k in range(1, STRIPS):
        y_copy(k).wait_send()
        h_copy(k).wait_send()
    for bank in range(BANKS):
        for copy in far_copies(bank) + near_copies(bank) + gather_near(bank) + gather_far(bank):
            copy.wait_send()
        x_copy(bank).wait_send()
        for copy in edge_copies(remote, bank, edge_send, edge_recv, edge_s, edge_r, before, after):
            copy.wait_send()
    dual_copy.wait()
    image_copy.wait()


def edge_copies(remote, bank, edge_send, edge_recv, edge_s, edge_r, before, after):
    return [
        remote(
            edge_send.at[bank, side], edge_recv.at[bank, side],
            edge_s.at[2 * bank + side], edge_r.at[2 * bank + side], (before, after)[side],
        )
        for side in range(2)
    ]


def per_device(constants, image, dual_coeffs, block_ids, block_counts, block_weights, block_data):
    any_space = pl.BlockSpec(memory_space=pl.ANY)
    in_vmem = pl.BlockSpec(memory_space=pltpu.VMEM)
    dma = lambda n: pltpu.SemaphoreType.DMA((n,))
    vmem = pltpu.VMEM
    image_new, dual_new = pl.pallas_call(
        kernel,
        out_shape=(
            jax.ShapeDtypeStruct((ROWS, PIX), F32),
            jax.ShapeDtypeStruct((BANKS, ROWS, PIX), BF16),
        ),
        in_specs=[any_space, any_space, in_vmem, in_vmem] + [any_space] * 9,
        out_specs=(any_space, any_space),
        scratch_shapes=[
            vmem((PAD, PIX), F32),
            vmem((PAD, PIX + 256), BF16),
            vmem((BANKS, ROWS, PIX), BF16),
            vmem((32, 32, 128), BF16),
            vmem((2, 32, 32, 128), BF16),
            vmem((8, 32, 1024), F32),
            vmem((512, 1024), BF16),
            vmem((512, 128), F32),
            vmem((384, 256), BF16),
            vmem((BANKS, ROWS, PAD), BF16),
            vmem((BANKS, ROWS, PAD), BF16),
            vmem((768, 128), BF16),
            vmem((2, 1024, 1024), BF16),
            vmem((2, ROWS, 1024), BF16),
            vmem((STRIPS, ROWS, 256), F32),
            vmem((PIX, 256), F32),
            vmem((PIX, 256), F32),
            vmem((STRIPS, ROWS, 256), F32),
            vmem((BANKS, PAD, PIX), BF16),
            vmem((BANKS, ROWS, PIX), F32),
            vmem((BANKS, ROWS, PIX), F32),
            vmem((BANKS, 2, QUARTER, PIX), F32),
            vmem((BANKS, 2, 16, PIX), F32),
            vmem((BANKS, QUARTER, PIX), F32),
            vmem((BANKS, QUARTER, PIX), F32),
            vmem((BANKS, ROWS, PIX), F32),
            vmem((BANKS, PAD, PIX), F32),
            vmem((BANKS, 2, RIM, PIX), F32),
            vmem((BANKS, 2, RIM, PIX), F32),
            vmem((BANKS, ROWS, PIX + 256), BF16),
            vmem((ROWS, PIX), F32),
            vmem((4, 1024, 128), F32),
            vmem((2, 4, 512, 256), BF16),
            vmem((4, 1024, 512), BF16),
            vmem((4, 1024, 512), BF16),
            vmem((2, ROWS, 1024), BF16),
            vmem((ROWS, PIX), F32),
            vmem((BANKS, ROWS, PIX), BF16),
            dma(11), dma(16), dma(16), dma(16), dma(16), dma(2), dma(2), dma(4), dma(4),
            dma(4), dma(4), dma(4), dma(4), dma(2), dma(2), dma(4), dma(4), dma(4), dma(4), dma(2),
        ],
        compiler_params=pltpu.CompilerParams(
            collective_id=0, has_side_effects=True, vmem_limit_bytes=60 * 1024 * 1024
        ),
    )(
        image[0],
        dual_coeffs[:, 0],
        jnp.broadcast_to(block_ids, (8, 32)),
        jnp.broadcast_to(block_counts, (8, 32)),
        block_weights[0],
        block_data[0],
        *constants,
    )
    return image_new[None], dual_new[:, None]


def solution(mesh):
    constants = tuple(jnp.asarray(c) for c in make_constants())

    def body(*args):
        return per_device(constants, *args)

    return jax.shard_map(
        body,
        mesh=mesh,
        in_specs=(
            P("chan", "strip", None),
            P(None, "chan", "strip", None),
            P("chan", "strip"),
            P("chan", "strip"),
            P("chan", "strip", None, None),
            P("chan", None, "strip", None, None),
        ),
        out_specs=(P("chan", "strip", None), P(None, "chan", "strip", None)),
        check_vma=False,
    )
```

profile of v0, /device:TPU:0, one launch (start us, length us, event | category | flops | bytes accessed | tf_op | source)
XLA Modules:
  0.0 96.8 jit_solution(15656156020141833597)
XLA Ops:
  1.3 0.0 copy-start.1
  1.3 0.6 broadcast_in_dim.23.counts_ref
  1.9 0.1 copy-done.1
  1.9 0.6 broadcast_in_dim.21.ids_ref
  2.5 90.9 %shard_map.140 = (f32[128,2048]{1,0:T(8,128)}, bf16[2,128,2048]{2,1,0:T(8,128)(2,1)}) custom-call(f32[128,2048]{1,0:T(8,128)} %bitcast.13, bf16[2,128,2048]{2,1,0:T(8,128)(2,1)} %bitcast.14, s32[8,32]{1,0:T(8,128)} %broadcast_in_dim.21.ids_ref, s32[8,32]{1,0:T(8,128)} %broadcast_in_dim.23.counts_ref, bf16[32,32,128]{2,1,0:T(8,128)(2,1)} %bitcast.16, ...), custom_call_target="tpu_custom_call" | custom-call | tf_op jit(solution)/shard_map/pallas_call | solution.py:567
  93.4 0.0 copy-start
  93.4 2.4 %copy.19 = f32[1,128,2048]{2,1,0:T(8,128)} copy(f32[1,128,2048]{2,1,0:T(8,128)} %bitcast.12) | data formatting | bytes 2097152
  95.8 0.0 copy-done
  95.8 1.0 %copy.20 = bf16[2,1,128,2048]{3,2,1,0:T(8,128)(2,1)} copy(bf16[2,1,128,2048]{3,2,1,0:T(8,128)(2,1)S(1)} %bitcast.11) | data formatting | bytes 2097152
Async XLA Ops:
  1.3 0.7 copy-start.1
  93.4 2.4 %copy-start = (bf16[2,128,2048]{2,1,0:T(8,128)(2,1)S(1)}, bf16[2,128,2048]{2,1,0:T(8,128)(2,1)}, u32[]{:S(2)}) copy-start(bf16[2,128,2048]{2,1,0:T(8,128)(2,1)} %get-tuple-element.5) | copy-start | bytes 3145732
where the time goes:
time: 97 us; the launch traced here: 96.8 us
  Pallas kernels  90.9 us (94%)
  local copies, waits for them, and re-layouts  4.6 us (5%)
  between operations  1.3 us (1%)
    pallas_call x1, Pallas kernels, per_device(): pl.pallas_call(kernel, out_shape=(jax.ShapeDtypeStruct((ROWS, PIX), F32),...  90.9 us
    unnamed x6, local copies, waits for them, and re-layouts  3.41 us

commit v1 on v0

--- a/solution.py
+++ b/solution.py
@@ -18,6 +18,11 @@
 PAD = ROWS + 2 * RIM
 BANKS = 2
 QUARTER = ROWS // 4
+FAR_FIRST = [
+    (dx, dy, core)
+    for dx, dy in ((1, 2), (0, 2), (1, 1), (1, 3), (0, 1), (0, 3), (1, 0))
+    for core in (0, 1)
+] + [(0, 0, 1)]
 
 root_three = math.sqrt(3.0)
 sqrt_two = math.sqrt(2.0)
@@ -103,14 +108,6 @@
     return jnp.dot(a, b, preferred_element_type=F32)
 
 
-def swap_halves(values):
-    tiles = [
-        pltpu.roll(values[:, 128 * t : 128 * t + 128], 64, 1)
-        for t in range(values.shape[1] // 128)
-    ]
-    return jnp.concatenate(tiles, axis=1) if len(tiles) > 1 else tiles[0]
-
-
 def lanes(shape):
     return lax.broadcasted_iota(jnp.int32, shape, len(shape) - 1)
 
@@ -121,6 +118,11 @@
         return carry
 
     lax.fori_loop(0, count, step, 0)
+
+
+def peer_at(me, k):
+    dx, dy, core = FAR_FIRST[k]
+    return ((me // 8 + dx) % 2) * 8 + (((me // 2) % 4 + dy) % 4) * 2 + (me + core) % 2
 
 
 def at(i, width):
@@ -204,32 +206,33 @@
     left, right = xpad[RIM : RIM + ROWS, 0:1024], xpad[RIM : RIM + ROWS, 1024:2048]
     folded[0] = (left + right).astype(BF16)
     folded[1] = (left - right).astype(BF16)
-    for parity in range(2):
+    lane = lanes((ROWS, 128))
+    edge_lane = (lane == 0) | (lane == 64)
+
+    def y_copy(e, k):
+        q = peer_at(me, k)
+        return remote(ysend.at[e, q], yrecv.at[e, at(me, ROWS)], y_s.at[e, k], y_r.at[e, k], {"strip": q})
+
+    for e in range(2):
         for pair in range(4):
-            tiles = dot(folded[parity], basis[parity, :, 256 * pair : 256 * pair + 256])
+            tiles = dot(folded[e], basis[e, :, 256 * pair : 256 * pair + 256])
             for half in range(2):
                 tile = tiles[:, 128 * half : 128 * half + 128]
                 p = 2 * pair + half
-                ysend[p, :, 128 * parity : 128 * parity + 128] = tile
-                if parity == 1:
-                    ysend[15 - p, :, 128:256] = tile
-    lane = lanes((ROWS, 128))
-    edge_lane = (lane == 0) | (lane == 64)
-    first = ysend[0, :, 0:128]
-    for p in range(7):
-        ysend[15 - p, :, 0:128] = jnp.where(edge_lane, ysend[p + 1, :, 0:128], ysend[p, :, 0:128])
-    ysend[8, :, 0:128] = jnp.where(
-        lane == 0, pltpu.roll(first, 64, 1), jnp.where(lane == 64, 0.0, ysend[7, :, 0:128])
-    )
-    ysend[0, :, 0:128] = jnp.where(lane == 64, 0.0, first)
-
-    def y_copy(k):
-        q = (me + k) % STRIPS
-        return remote(ysend.at[q], yrecv.at[at(me, ROWS)], y_s.at[k], y_r.at[k], {"strip": q})
-
-    for k in range(1, STRIPS):
-        y_copy(k).start()
-    yrecv[at(me, ROWS), :] = ysend[me]
+                ysend[e, p] = tile
+                if e == 1:
+                    ysend[e, 15 - p] = tile
+        if e == 0:
+            first = ysend[0, 0]
+            for p in range(7):
+                ysend[0, 15 - p] = jnp.where(edge_lane, ysend[0, p + 1], ysend[0, p])
+            ysend[0, 8] = jnp.where(
+                lane == 0, pltpu.roll(first, 64, 1), jnp.where(lane == 64, 0.0, ysend[0, 7])
+            )
+            ysend[0, 0] = jnp.where(lane == 64, 0.0, first)
+        for k in range(15):
+            y_copy(e, k).start()
+        yrecv[e, at(me, ROWS), :] = ysend[e, me]
 
     for copy in halos:
         copy.wait_recv()
@@ -241,13 +244,14 @@
     outside = ((row < RIM) & (me == 0)) | ((row >= RIM + ROWS) & (me == STRIPS - 1))
     xwide[:, 128 : 128 + PIX] = jnp.where(outside, 0.0, xpad[...]).astype(BF16)
 
-    def analyse_columns(t):
-        start = pl.multiple_of(t * 128, 128)
-        both = dot(xwide[:, pl.ds(start, 384)], ana_cols[...]).astype(BF16)
-        coeffs[0, :, pl.ds(start, 128)] = both[:, 0:128]
-        coeffs[1, :, pl.ds(start, 128)] = both[:, 128:256]
-
-    loop(16, analyse_columns)
+    def analyse_columns(i):
+        for t in range(4):
+            start = pl.multiple_of(i * 512 + t * 128, 128)
+            both = dot(xwide[:, pl.ds(start, 384)], ana_cols[...]).astype(BF16)
+            coeffs[0, :, pl.ds(start, 128)] = both[:, 0:128]
+            coeffs[1, :, pl.ds(start, 128)] = both[:, 128:256]
+
+    loop(4, analyse_columns)
 
     def far_copies(bank):
         return [
@@ -292,13 +296,14 @@
         ]
 
     for bank in range(BANKS):
-        def analyse_rows(t, bank=bank):
-            cols = at(t, 512)
-            values = dual[bank, :, cols].astype(F32) + dot(ana_rows[bank], coeffs[bank, :, cols])
-            trial[bank, :, cols] = values
-            squares[bank, :, cols] = values * values
-
-        loop(4, analyse_rows)
+        def analyse_rows(i, bank=bank):
+            for t in range(4):
+                cols = pl.ds(pl.multiple_of(i * 1024 + t * 256, 256), 256)
+                values = dual[bank, :, cols].astype(F32) + dot(ana_rows[bank], coeffs[bank, :, cols])
+                trial[bank, :, cols] = values
+                squares[bank, :, cols] = values * values
+
+        loop(2, analyse_rows)
         for copy in far_copies(bank):
             copy.start()
 
@@ -327,7 +332,8 @@
 
     loop(4, pick_columns)
     slot = lanes((8, 32))
-    live_ids = jnp.where(slot < counts_ref[...], ids_ref[...], -1).astype(F32).astype(BF16)
+    ids = jnp.broadcast_to(ids_ref[...], (8, 32))
+    live_ids = jnp.where(slot < counts_ref[...], ids, -1).astype(F32).astype(BF16)
     spread = jnp.where(
         lanes((32, 256)) // 8 == lax.broadcasted_iota(jnp.int32, (32, 256), 0), 1.0, 0.0
     ).astype(BF16)
@@ -346,7 +352,9 @@
                 ],
                 axis=1,
             ).astype(BF16)
-            wd_dense[kind, u] = dot(place, picked).astype(BF16)
+            spread_out = dot(place, picked).astype(BF16)
+            wd_dense[kind, 0, u] = spread_out[:, 0:128]
+            wd_dense[kind, 1, u] = spread_out[:, 128:256]
 
     for bank in range(BANKS):
         for copy in far_copies(bank):
@@ -363,84 +371,84 @@
         quarter_sum[bank] = squares[bank, at(z, QUARTER), :] + near[bank, 0] + near[bank, 1]
         x_copy(bank).start()
 
-    lane_sign = jnp.where((lanes((1, 256)) // 64) % 2 == 0, -sign, sign).astype(F32)
-    for k in range(1, STRIPS):
-        y_copy(k).wait_recv()
-
-    def fold_rows(i):
-        rows = at(i, 64)
-        low = pl.ds(pl.multiple_of(512 + i * 64, 64), 64)
-        y0, y1, y2, y3 = (
-            yrecv[pl.ds(pl.multiple_of(512 * j + i * 64, 64), 64), :] for j in range(4)
-        )
-        tw = twiddle[rows, :]
-        c1, s1, c2, s2, c3, s3 = (tw[:, j : j + 1] for j in range(6))
-        sum_a, sum_b, dif_a, dif_b = y0 + y2, y1 + y3, y0 - y2, y1 - y3
-        forward[0, rows, 0:256] = (sum_a + sum_b).astype(BF16)
-        alt = sum_a - sum_b
-        parts = (
-            (c1 * dif_a - s1 * dif_b, -c1 * dif_b - s1 * dif_a),
-            (c2 * alt, -s2 * alt),
-            (c3 * dif_a + s3 * dif_b, c3 * dif_b - s3 * dif_a),
-        )
-        for u, (real, imag) in enumerate(parts, 1):
-            real, imag = real.astype(BF16), imag.astype(BF16)
-            forward[u, rows, 0:256] = real
-            forward[u, low, 0:256] = imag
-            forward[u, rows, 256:512] = imag
-            forward[u, low, 256:512] = -real
-
-    loop(8, fold_rows)
-
-    for u in range(4):
-        def weigh(m, u=u):
-            rows = at(m, 128)
-            low = pl.ds(pl.multiple_of(512 + m * 128, 128), 128)
-            if u == 0:
-                real = dot(fourier[rows, 0:512], forward[0, 0:512, 0:256])
-                imag = -dot(fourier[rows, 512:1024], forward[0, 0:512, 0:256])
-            else:
-                both = dot(fourier[rows, :], forward[u])
-                real, imag = both[:, 0:256], both[:, 256:512]
-            spectrum = real + lane_sign * swap_halves(imag)
-            weight = wd_dense[0, u, rows, :].astype(F32)
-            residual = weight * (weight * spectrum - wd_dense[1, u, rows, :].astype(F32))
-            turned = (lane_sign * swap_halves(residual)).astype(BF16)
-            residual = residual.astype(BF16)
-            backward[u, rows, 0:256] = residual
-            backward[u, low, 0:256] = turned
-            if u > 0:
-                backward[u, rows, 256:512] = -turned
-                backward[u, low, 256:512] = residual
-
-        loop(4, weigh)
-
-    def unfold_rows(m):
-        rows = at(m, 128)
-        left_side = fourier[rows, :]
-        tw = twiddle[rows, :]
-        c1, s1, c2, s2, c3, s3 = (tw[:, j : j + 1] for j in range(6))
-        k0 = dot(left_side, backward[0, :, 0:256])
-        k1, k2, k3 = (dot(left_side, backward[u]) for u in (1, 2, 3))
-        r1 = c1 * k1[:, 0:256] - s1 * k1[:, 256:512]
-        i1 = c1 * k1[:, 256:512] + s1 * k1[:, 0:256]
-        r2 = c2 * k2[:, 0:256] - s2 * k2[:, 256:512]
-        r3 = c3 * k3[:, 0:256] - s3 * k3[:, 256:512]
-        i3 = c3 * k3[:, 256:512] + s3 * k3[:, 0:256]
-        plus, minus, real, imag = k0 + r2, k0 - r2, r1 + r3, i3 - i1
-        for j, value in enumerate((plus + real, minus + imag, plus - real, minus - imag)):
-            hsend[pl.ds(pl.multiple_of(512 * j + m * 128, 128), 128), :] = value
-
-    loop(4, unfold_rows)
-
-    def h_copy(k):
-        q = (me + k) % STRIPS
-        return remote(hsend.at[at(q, ROWS)], hrecv.at[me], h_s.at[k], h_r.at[k], {"strip": q})
-
-    for k in range(1, STRIPS):
-        h_copy(k).start()
-    hrecv[me] = hsend[at(me, ROWS), :]
-
+    lane_sign = jnp.where(lanes((1, 128)) < 64, -sign, sign).astype(F32)
+
+    def times_i(values):
+        return lane_sign * pltpu.roll(values, 64, 1)
+
+    def h_copy(e, k):
+        q = peer_at(me, k)
+        return remote(hsend.at[e, at(q, ROWS)], hrecv.at[e, me], h_s.at[e, k], h_r.at[e, k], {"strip": q})
+
+    def column_stage(e):
+        for k in range(15):
+            y_copy(e, k).wait_recv()
+
+        def fold_rows(i):
+            for part in range(2):
+                start = i * 128 + part * 64
+                rows = pl.ds(pl.multiple_of(start, 64), 64)
+                low = pl.ds(pl.multiple_of(512 + start, 64), 64)
+                y0, y1, y2, y3 = (
+                    yrecv[e, pl.ds(pl.multiple_of(512 * j + start, 64), 64), :] for j in range(4)
+                )
+                tw = twiddle[rows, :]
+                sum_a, sum_b, dif_a, dif_b = y0 + y2, y1 + y3, y0 - y2, y1 - y3
+                total, alt = sum_a + sum_b, sum_a - sum_b
+                turned_a, turned_b = times_i(dif_a), times_i(dif_b)
+                folds = (
+                    (total, times_i(total)),
+                    (dif_a - turned_b, turned_a + dif_b),
+                    (alt, times_i(alt)),
+                    (dif_a + turned_b, turned_a - dif_b),
+                )
+                for u, (value, turned) in enumerate(folds):
+                    if u > 0:
+                        cos, sin = tw[:, 2 * u - 2 : 2 * u - 1], tw[:, 2 * u - 1 : 2 * u]
+                        value, turned = cos * value - sin * turned, cos * turned + sin * value
+                    lanes_of = slice(128 * (u % 2), 128 * (u % 2) + 128)
+                    forward[u // 2, rows, lanes_of] = value.astype(BF16)
+                    forward[u // 2, low, lanes_of] = (-turned).astype(BF16)
+
+        loop(4, fold_rows)
+        for pair in range(2):
+            for m in range(2):
+                rows, low = slice(256 * m, 256 * m + 256), slice(512 + 256 * m, 768 + 256 * m)
+                both = dot(fourier[rows, :], forward[pair])
+                for half in range(2):
+                    u = 2 * pair + half
+                    spectrum = both[:, 128 * half : 128 * half + 128]
+                    weight = wd_dense[0, e, u, rows, :].astype(F32)
+                    residual = weight * (weight * spectrum - wd_dense[1, e, u, rows, :].astype(F32))
+                    turned = times_i(residual).astype(BF16)
+                    residual = residual.astype(BF16)
+                    backward[u, rows, 0:128] = residual
+                    backward[u, low, 0:128] = turned
+                    if u > 0:
+                        backward[u, rows, 128:256] = turned
+                        backward[u, low, 128:256] = -residual
+        for m in range(4):
+            rows = slice(128 * m, 128 * m + 128)
+            left_side = fourier[rows, :]
+            tw = twiddle[rows, :]
+            terms = [dot(left_side, backward[0, :, 0:128])]
+            for u in (1, 2, 3):
+                both = dot(left_side, backward[u])
+                cos, sin = tw[:, 2 * u - 2 : 2 * u - 1], tw[:, 2 * u - 1 : 2 * u]
+                value, turned = both[:, 0:128], both[:, 128:256]
+                terms.append(cos * value + sin * turned)
+                if u == 1:
+                    turned_odd = cos * turned - sin * value
+                if u == 3:
+                    turned_odd = turned_odd - (cos * turned - sin * value)
+            plus, minus, odd = terms[0] + terms[2], terms[0] - terms[2], terms[1] + terms[3]
+            for j, value in enumerate((plus + odd, minus + turned_odd, plus - odd, minus - turned_odd)):
+                hsend[e, 512 * j + 128 * m : 512 * j + 128 * m + 128, :] = value
+        for k in range(15):
+            h_copy(e, k).start()
+        hrecv[e, me] = hsend[e, at(me, ROWS), :]
+
+    column_stage(0)
     bound = shrink_level * math.sqrt(8.0)
     for bank in range(BANKS):
         x_copy(bank).wait_recv()
@@ -448,6 +456,7 @@
         factor[bank, at(z, QUARTER), :] = bound / jnp.maximum(jnp.sqrt(total), bound)
         for copy in gather_near(bank):
             copy.start()
+    column_stage(1)
     for bank in range(BANKS):
         for copy in gather_near(bank):
             copy.wait_recv()
@@ -485,35 +494,40 @@
         synth_wide[bank, :, 0:128] = jnp.zeros((ROWS, 128), BF16)
         synth_wide[bank, :, 128 + PIX : 256 + PIX] = jnp.zeros((ROWS, 128), BF16)
 
-        def synthesise_rows(t, bank=bank):
-            values = dot(syn_rows[bank], combined[bank, :, at(t, 512)].astype(BF16))
-            synth_wide[bank, :, pl.ds(pl.multiple_of(128 + t * 512, 128), 512)] = values.astype(BF16)
-
-        loop(4, synthesise_rows)
-
-    def synthesise_columns(t):
-        start = pl.multiple_of(t * 128, 128)
-        window = pl.ds(start, 384)
-        adjoint[:, pl.ds(start, 128)] = dot(synth_wide[0, :, window], syn_cols[0:384]) + dot(
-            synth_wide[1, :, window], syn_cols[384:768]
-        )
-
-    loop(16, synthesise_columns)
-
-    for k in range(1, STRIPS):
-        h_copy(k).wait_recv()
-    for p in range(8):
-        own = hrecv[p, :, 0:128]
-        if p == 0:
-            even = jnp.where(
-                lane == 0, own,
-                jnp.where(lane == 64, pltpu.roll(hrecv[8, :, 0:128], 64, 1), own + hrecv[15, :, 0:128]),
+        def synthesise_rows(i, bank=bank):
+            for t in range(4):
+                start = i * 1024 + t * 256
+                cols = pl.ds(pl.multiple_of(start, 256), 256)
+                values = dot(syn_rows[bank], combined[bank, :, cols].astype(BF16))
+                synth_wide[bank, :, pl.ds(pl.multiple_of(128 + start, 128), 256)] = values.astype(BF16)
+
+        loop(2, synthesise_rows)
+
+    def synthesise_columns(i):
+        for t in range(4):
+            start = pl.multiple_of(i * 512 + t * 128, 128)
+            window = pl.ds(start, 384)
+            adjoint[:, pl.ds(start, 128)] = dot(synth_wide[0, :, window], syn_cols[0:384]) + dot(
+                synth_wide[1, :, window], syn_cols[384:768]
             )
-        else:
-            even = own + jnp.where(edge_lane, hrecv[16 - p, :, 0:128], hrecv[15 - p, :, 0:128])
-        odd = hrecv[p, :, 128:256] + hrecv[15 - p, :, 128:256]
-        packed[0, :, 128 * p : 128 * p + 128] = even.astype(BF16)
-        packed[1, :, 128 * p : 128 * p + 128] = odd.astype(BF16)
+
+    loop(4, synthesise_columns)
+
+    for e in range(2):
+        for k in range(15):
+            h_copy(e, k).wait_recv()
+        for p in range(8):
+            value = hrecv[e, p]
+            if e == 1:
+                value = value + hrecv[e, 15 - p]
+            elif p == 0:
+                value = jnp.where(
+                    lane == 0, value,
+                    jnp.where(lane == 64, pltpu.roll(hrecv[0, 8], 64, 1), value + hrecv[0, 15]),
+                )
+            else:
+                value = value + jnp.where(edge_lane, hrecv[0, 16 - p], hrecv[0, 15 - p])
+            packed[e, :, 128 * p : 128 * p + 128] = value.astype(BF16)
 
     def finish(i):
         cols = at(i, 256)
@@ -536,9 +550,10 @@
 
     for copy in halos:
         copy.wait_send()
-    for k in range(1, STRIPS):
-        y_copy(k).wait_send()
-        h_copy(k).wait_send()
+    for e in range(2):
+        for k in range(15):
+            y_copy(e, k).wait_send()
+            h_copy(e, k).wait_send()
     for bank in range(BANKS):
         for copy in far_copies(bank) + near_copies(bank) + gather_near(bank) + gather_far(bank):
             copy.wait_send()
@@ -562,7 +577,7 @@
 def per_device(constants, image, dual_coeffs, block_ids, block_counts, block_weights, block_data):
     any_space = pl.BlockSpec(memory_space=pl.ANY)
     in_vmem = pl.BlockSpec(memory_space=pltpu.VMEM)
-    dma = lambda n: pltpu.SemaphoreType.DMA((n,))
+    dma = lambda *n: pltpu.SemaphoreType.DMA(n)
     vmem = pltpu.VMEM
     image_new, dual_new = pl.pallas_call(
         kernel,
@@ -587,10 +602,10 @@
             vmem((768, 128), BF16),
             vmem((2, 1024, 1024), BF16),
             vmem((2, ROWS, 1024), BF16),
-            vmem((STRIPS, ROWS, 256), F32),
-            vmem((PIX, 256), F32),
-            vmem((PIX, 256), F32),
-            vmem((STRIPS, ROWS, 256), F32),
+            vmem((2, STRIPS, ROWS, 128), F32),
+            vmem((2, PIX, 128), F32),
+            vmem((2, PIX, 128), F32),
+            vmem((2, STRIPS, ROWS, 128), F32),
             vmem((BANKS, PAD, PIX), BF16),
             vmem((BANKS, ROWS, PIX), F32),
             vmem((BANKS, ROWS, PIX), F32),
@@ -605,13 +620,13 @@
             vmem((BANKS, ROWS, PIX + 256), BF16),
             vmem((ROWS, PIX), F32),
             vmem((4, 1024, 128), F32),
-            vmem((2, 4, 512, 256), BF16),
-            vmem((4, 1024, 512), BF16),
-            vmem((4, 1024, 512), BF16),
+            vmem((2, 2, 4, 512, 128), BF16),
+            vmem((2, 1024, 256), BF16),
+            vmem((4, 1024, 256), BF16),
             vmem((2, ROWS, 1024), BF16),
             vmem((ROWS, PIX), F32),
             vmem((BANKS, ROWS, PIX), BF16),
-            dma(11), dma(16), dma(16), dma(16), dma(16), dma(2), dma(2), dma(4), dma(4),
+            dma(11), dma(2, 15), dma(2, 15), dma(2, 15), dma(2, 15), dma(2), dma(2), dma(4), dma(4),
             dma(4), dma(4), dma(4), dma(4), dma(2), dma(2), dma(4), dma(4), dma(4), dma(4), dma(2),
         ],
         compiler_params=pltpu.CompilerParams(
@@ -620,8 +635,8 @@
     )(
         image[0],
         dual_coeffs[:, 0],
-        jnp.broadcast_to(block_ids, (8, 32)),
-        jnp.broadcast_to(block_counts, (8, 32)),
+        block_ids,
+        block_counts,
         block_weights[0],
         block_data[0],
         *constants,

time: 97 us -> 81.1 us (0.84)
  Pallas kernels: 90.9 us -> 76.3 us
  local copies, waits for them, and re-layouts: 4.6 us -> 3.36 us
    pallas_call x1, Pallas kernels: 90.9 us -> 76.3 us  [per_device(): pl.pallas_call(kernel, out_shape=(jax.ShapeDtypeStruct((ROWS, PIX), F32),...]
    broadcast_in_dim x2 -> x0, local copies, waits for them, and re-layouts: 1.19 us -> none  [the longest x1 0.6 us: per_device(): jnp.broadcast_to(block_counts, (8, 32))]
    unnamed x6 -> x4, local copies, waits for them, and re-layouts: 3.41 us -> 3.36 us
where the time goes in v1:
time: 81.1 us; the launch traced here: 81 us
  Pallas kernels  76.3 us (94%)
  local copies, waits for them, and re-layouts  3.36 us (4%)
  between operations  1.29 us (2%)
    pallas_call x1, Pallas kernels, per_device(): pl.pallas_call(kernel, out_shape=(jax.ShapeDtypeStruct((ROWS, PIX), F32),...  76.3 us
    unnamed x4, local copies, waits for them, and re-layouts  3.36 us

profile of v1, /device:TPU:0, one launch (start us, length us, event | category | flops | bytes accessed | tf_op | source)
XLA Modules:
  0.0 81.0 jit_solution(5114568978901627471)
XLA Ops:
  1.3 76.3 %shard_map.140 = (f32[128,2048]{1,0:T(8,128)}, bf16[2,128,2048]{2,1,0:T(8,128)(2,1)}) custom-call(f32[128,2048]{1,0:T(8,128)} %bitcast.8, bf16[2,128,2048]{2,1,0:T(8,128)(2,1)} %bitcast.9, s32[1,32]{1,0:T(1,128)} %ids_ref.1, s32[1,1]{1,0:T(1,128)S(6)} %copy.18.counts_ref, bf16[32,32,128]{2,1,0:T(8,128)(2,1)} %bitcast.13, bf16[2,32,32,128]{3,2,1,0:T(8,128)(2,1)} %bitcast.12, ...), custom_call_target="tpu_custom_call" | custom-call | tf_op jit(solution)/shard_map/pallas_call | solution.py:582
  77.6 0.0 copy-start
  77.6 2.4 %copy.19 = f32[1,128,2048]{2,1,0:T(8,128)} copy(f32[1,128,2048]{2,1,0:T(8,128)} %bitcast.11) | data formatting | bytes 2097152
  80.0 0.0 copy-done
  80.0 1.0 %copy.20 = bf16[2,1,128,2048]{3,2,1,0:T(8,128)(2,1)} copy(bf16[2,1,128,2048]{3,2,1,0:T(8,128)(2,1)S(1)} %bitcast.10) | data formatting | bytes 2097152
Async XLA Ops:
  77.6 2.4 %copy-start = (bf16[2,128,2048]{2,1,0:T(8,128)(2,1)S(1)}, bf16[2,128,2048]{2,1,0:T(8,128)(2,1)}, u32[]{:S(2)}) copy-start(bf16[2,128,2048]{2,1,0:T(8,128)(2,1)} %get-tuple-element.5) | copy-start | bytes 3145732

commit v2 on v1

--- a/solution.py
+++ b/solution.py
@@ -135,10 +135,11 @@
     image_out, dual_out,
     xpad, xwide, dual, weights, data, tables, fourier, twiddle, ana_cols, ana_rows, syn_rows, syn_cols,
     basis, folded, ysend, yrecv, hsend, hrecv, coeffs, trial, squares, near, far, quarter_sum, other_sum,
-    factor, combined, edge_send, edge_recv, synth_wide, adjoint, wd_flat, wd_dense, forward, backward,
-    packed, image_new, dual_new,
+    factor, combined, edge_send, edge_recv, synth_wide, adjoint, own_flat, other_flat, rim_flat,
+    w_send, w_recv, d_send, d_recv, ids_send, ids_recv, rim_send, rim_recv, wd_dense,
+    forward, kept, backward, packed, image_new, dual_new,
     local_sem, y_s, y_r, h_s, h_r, halo_s, halo_r, edge_s, edge_r, far_s, far_r, near_s, near_r,
-    x_s, x_r, ga_s, ga_r, gb_s, gb_r, out_sem,
+    x_s, x_r, ga_s, ga_r, gb_s, gb_r, swap_s, swap_r, out_sem,
 ):
     me = lax.axis_index("strip")
     chan = lax.axis_index("chan")
@@ -155,8 +156,8 @@
         pltpu.make_async_copy(src, dst, local_sem.at[i])
         for i, (src, dst) in enumerate(
             [
+                (tables_hbm, tables),
                 (image_hbm, xpad.at[RIM : RIM + ROWS]),
-                (tables_hbm, tables),
                 (ana_cols_hbm, ana_cols),
                 (ana_rows_hbm, ana_rows),
                 (dual_hbm, dual),
@@ -191,10 +192,6 @@
         remote(xpad.at[ROWS : RIM + ROWS], xpad.at[0:RIM], halo_s.at[1], halo_r.at[1], after),
     ]
     loads[0].wait()
-    for copy in halos:
-        copy.start()
-
-    loads[1].wait()
     for parity in range(2):
         def make_basis(i, parity=parity):
             coarse_cos = tables[4 * parity, pl.ds(i, 1), :]
@@ -203,36 +200,25 @@
             basis[parity, at(i, 32), :] = block.astype(BF16)
 
         loop(32, make_basis)
+    loads[1].wait()
+    for copy in halos:
+        copy.start()
     left, right = xpad[RIM : RIM + ROWS, 0:1024], xpad[RIM : RIM + ROWS, 1024:2048]
     folded[0] = (left + right).astype(BF16)
     folded[1] = (left - right).astype(BF16)
-    lane = lanes((ROWS, 128))
-    edge_lane = (lane == 0) | (lane == 64)
-
-    def y_copy(e, k):
+    def y_copy(k):
         q = peer_at(me, k)
-        return remote(ysend.at[e, q], yrecv.at[e, at(me, ROWS)], y_s.at[e, k], y_r.at[e, k], {"strip": q})
+        return remote(ysend.at[q], yrecv.at[at(me, ROWS)], y_s.at[k], y_r.at[k], {"strip": q})
 
     for e in range(2):
         for pair in range(4):
             tiles = dot(folded[e], basis[e, :, 256 * pair : 256 * pair + 256])
             for half in range(2):
-                tile = tiles[:, 128 * half : 128 * half + 128]
                 p = 2 * pair + half
-                ysend[e, p] = tile
-                if e == 1:
-                    ysend[e, 15 - p] = tile
-        if e == 0:
-            first = ysend[0, 0]
-            for p in range(7):
-                ysend[0, 15 - p] = jnp.where(edge_lane, ysend[0, p + 1], ysend[0, p])
-            ysend[0, 8] = jnp.where(
-                lane == 0, pltpu.roll(first, 64, 1), jnp.where(lane == 64, 0.0, ysend[0, 7])
-            )
-            ysend[0, 0] = jnp.where(lane == 64, 0.0, first)
-        for k in range(15):
-            y_copy(e, k).start()
-        yrecv[e, at(me, ROWS), :] = ysend[e, me]
+                ysend[15 - p if e else p] = tiles[:, 128 * half : 128 * half + 128]
+    for k in range(15):
+        y_copy(k).start()
+    yrecv[at(me, ROWS), :] = ysend[me]
 
     for copy in halos:
         copy.wait_recv()
@@ -309,124 +295,185 @@
 
     for i in (5, 6, 7, 8):
         loads[i].wait()
-    lane256 = lanes((128, 256))
-    column = 2 * (lane256 % 64) + lane256 // 128
-    column = jnp.where(me < 8, column, (128 - column) % 128)
-    hit = lax.broadcasted_iota(jnp.int32, (128, 256), 0) == column
-    imag_lane = (lane256 // 64) % 2 == 1
-    pick_both = jnp.where(hit, 1.0, 0.0).astype(BF16)
-    pick_real = jnp.where(hit & ~imag_lane, 1.0, 0.0).astype(BF16)
-    pick_imag = (jnp.where(hit & imag_lane, 1.0, 0.0) * sign.astype(F32)).astype(BF16)
-
-    def pick_columns(i):
-        rows = at(i, 256)
-        blocks = at(i, 8)
-        flat = (
-            dot(weights[blocks].reshape(256, 128), pick_both),
-            dot(data[0, blocks].reshape(256, 128), pick_real)
-            + dot(data[1, blocks].reshape(256, 128), pick_imag),
+    lane_of = lanes((128, 128))
+    half_lane = lane_of % 64
+    imag_lane = lane_of >= 64
+    column_row = lax.broadcasted_iota(jnp.int32, (128, 128), 0)
+    own_hit = column_row == jnp.where(me < 8, 2 * half_lane, 127 - 2 * half_lane)
+    other_hit = column_row == jnp.where(me < 8, 2 * half_lane + 1, 128 - 2 * half_lane)
+    one_hot = lambda mask: jnp.where(mask, 1.0, 0.0).astype(BF16)
+    signed = lambda mask: jnp.where(mask, sign.astype(F32), 0.0).astype(BF16)
+    own_real, own_imag = one_hot(own_hit & ~imag_lane), signed(own_hit & imag_lane)
+    other_real, other_imag = one_hot(other_hit & ~imag_lane), signed(other_hit & imag_lane)
+    other_low, other_high = one_hot(other_hit & ~imag_lane), one_hot(other_hit & imag_lane)
+    mirror = {"strip": 15 - me}
+    rim_peer = {"strip": jnp.where(me < 8, 8 + (8 - me) % 8, (16 - me) % 8)}
+
+    def picked_rows(ref, i):
+        return ref[8 * i : 8 * i + 8].reshape(256, 128)
+
+    for i in range(4):
+        rows = slice(256 * i, 256 * i + 256)
+        d_send[rows, :] = dot(picked_rows(data.at[0], i), other_real) + dot(
+            picked_rows(data.at[1], i), other_imag
         )
-        for kind in range(2):
-            for half in range(2):
-                wd_flat[2 * kind + half, rows, :] = flat[kind][:, 128 * half : 128 * half + 128]
-
-    loop(4, pick_columns)
+        if i < 2:
+            w_send[rows, :] = dot(picked_rows(weights, i), other_low) + dot(
+                picked_rows(weights, i + 2), other_high
+            )
     slot = lanes((8, 32))
     ids = jnp.broadcast_to(ids_ref[...], (8, 32))
     live_ids = jnp.where(slot < counts_ref[...], ids, -1).astype(F32).astype(BF16)
     spread = jnp.where(
         lanes((32, 256)) // 8 == lax.broadcasted_iota(jnp.int32, (32, 256), 0), 1.0, 0.0
     ).astype(BF16)
-    slot_ids = dot(live_ids, spread)[0:1, :].astype(jnp.int32)
+    ids_send[...] = dot(live_ids, spread)
+    sel_row, sel_lane = lax.broadcasted_iota(jnp.int32, (8, 128), 0), lanes((8, 128))
+    turn = (((1,), (1,)), ((), ()))
+    rim = 0.0
+    for i, values in enumerate((weights[...], data[0], data[1])):
+        select = one_hot((sel_row == i) & (sel_lane == 0))
+        rim = rim + lax.dot_general(select, values.reshape(1024, 128), turn, preferred_element_type=F32)
+    rim_send[...] = rim
+    swaps = [
+        remote(w_send, w_recv, swap_s.at[0], swap_r.at[0], mirror),
+        remote(ids_send, ids_recv.at[0], swap_s.at[1], swap_r.at[1], mirror),
+        remote(ids_send, ids_recv.at[1], swap_s.at[2], swap_r.at[2], rim_peer),
+        remote(rim_send, rim_recv, swap_s.at[3], swap_r.at[3], rim_peer),
+        remote(d_send.at[0:512], d_recv.at[0:512], swap_s.at[4], swap_r.at[4], mirror),
+        remote(d_send.at[512:1024], d_recv.at[512:1024], swap_s.at[5], swap_r.at[5], mirror),
+    ]
+    for copy in swaps[0:5]:
+        copy.start()
+
+    for i in range(4):
+        rows = slice(256 * i, 256 * i + 256)
+        own_flat[0, rows, :] = dot(picked_rows(weights, i), one_hot(own_hit))
+        own_flat[1, rows, :] = dot(picked_rows(data.at[0], i), own_real) + dot(
+            picked_rows(data.at[1], i), own_imag
+        )
     place_row = lax.broadcasted_iota(jnp.int32, (512, 256), 0)
-    place_col = lanes((512, 256))
-    place = jnp.where(
-        (slot_ids == place_row // 8) & (place_row % 8 == place_col % 8), 1.0, 0.0
-    ).astype(BF16)
-    for kind in range(2):
-        for u in range(4):
-            picked = jnp.concatenate(
-                [
-                    wd_flat[2 * kind, pl.ds(u, 256, stride=4), :],
-                    wd_flat[2 * kind + 1, pl.ds(u, 256, stride=4), :],
-                ],
-                axis=1,
-            ).astype(BF16)
-            spread_out = dot(place, picked).astype(BF16)
-            wd_dense[kind, 0, u] = spread_out[:, 0:128]
-            wd_dense[kind, 1, u] = spread_out[:, 128:256]
-
-    for bank in range(BANKS):
-        for copy in far_copies(bank):
-            copy.wait_recv()
-        low = pl.ds(pl.multiple_of(zp * QUARTER, QUARTER), 16)
-        high = pl.ds(pl.multiple_of(zm * QUARTER + 16, 16), 16)
-        squares[bank, low, :] = squares[bank, low, :] + far[bank, 0]
-        squares[bank, high, :] = squares[bank, high, :] + far[bank, 1]
-        for copy in near_copies(bank):
-            copy.start()
-    for bank in range(BANKS):
-        for copy in near_copies(bank):
-            copy.wait_recv()
-        quarter_sum[bank] = squares[bank, at(z, QUARTER), :] + near[bank, 0] + near[bank, 1]
-        x_copy(bank).start()
+    same_row = place_row % 8 == lanes((512, 256)) % 8
+
+    def place_of(slot_ids):
+        return one_hot((slot_ids[0:1, :].astype(jnp.int32) == place_row // 8) & same_row)
+
+    def by_row(flat_w, flat_d, u):
+        rows = pl.ds(u, 256, stride=4)
+        return jnp.concatenate([flat_w[rows, :], flat_d[rows, :]], axis=1).astype(BF16)
+
+    def put_dense(role, u, values):
+        values = values.astype(BF16)
+        wd_dense[role, 0, u] = values[:, 0:128]
+        wd_dense[role, 1, u] = values[:, 128:256]
+
+    own_place = place_of(ids_send[...])
+    for u in range(4):
+        put_dense(0, u, dot(own_place, by_row(own_flat.at[0], own_flat.at[1], u)))
 
     lane_sign = jnp.where(lanes((1, 128)) < 64, -sign, sign).astype(F32)
+    swap_halves = lambda values: pltpu.roll(values, 64, 1)
+    first_lane = (lanes((1, 128)) == 0) & (me == 0)
+    middle_lane = (lanes((1, 128)) == 64) & (me == 0)
 
     def times_i(values):
-        return lane_sign * pltpu.roll(values, 64, 1)
-
-    def h_copy(e, k):
+        return lane_sign * swap_halves(values)
+
+    def h_copy(k):
         q = peer_at(me, k)
-        return remote(hsend.at[e, at(q, ROWS)], hrecv.at[e, me], h_s.at[e, k], h_r.at[e, k], {"strip": q})
-
-    def column_stage(e):
-        for k in range(15):
-            y_copy(e, k).wait_recv()
-
-        def fold_rows(i):
-            for part in range(2):
-                start = i * 128 + part * 64
-                rows = pl.ds(pl.multiple_of(start, 64), 64)
-                low = pl.ds(pl.multiple_of(512 + start, 64), 64)
-                y0, y1, y2, y3 = (
-                    yrecv[e, pl.ds(pl.multiple_of(512 * j + start, 64), 64), :] for j in range(4)
-                )
-                tw = twiddle[rows, :]
+        return remote(hsend.at[at(q, ROWS)], hrecv.at[me], h_s.at[k], h_r.at[k], {"strip": q})
+
+    def fold_rows(i):
+        for part in range(2):
+            start = i * 128 + part * 64
+            rows = pl.ds(pl.multiple_of(start, 64), 64)
+            low = pl.ds(pl.multiple_of(512 + start, 64), 64)
+            loaded = [yrecv[pl.ds(pl.multiple_of(512 * j + start, 64), 64), :] for j in range(4)]
+            tw = twiddle[rows, :]
+            for role in range(2):
+                if role == 0:
+                    parts = [jnp.where(middle_lane, 0.0, y) for y in loaded]
+                else:
+                    parts = [
+                        jnp.where(first_lane, swap_halves(y), jnp.where(middle_lane, 0.0, y)) for y in loaded
+                    ]
+                unit = times_i if role == 0 else (lambda values: -times_i(values))
+                y0, y1, y2, y3 = parts
                 sum_a, sum_b, dif_a, dif_b = y0 + y2, y1 + y3, y0 - y2, y1 - y3
                 total, alt = sum_a + sum_b, sum_a - sum_b
-                turned_a, turned_b = times_i(dif_a), times_i(dif_b)
+                turned_a, turned_b = unit(dif_a), unit(dif_b)
                 folds = (
-                    (total, times_i(total)),
+                    (total, unit(total)),
                     (dif_a - turned_b, turned_a + dif_b),
-                    (alt, times_i(alt)),
+                    (alt, unit(alt)),
                     (dif_a + turned_b, turned_a - dif_b),
                 )
+                lanes_of = slice(128 * role, 128 * role + 128)
                 for u, (value, turned) in enumerate(folds):
                     if u > 0:
                         cos, sin = tw[:, 2 * u - 2 : 2 * u - 1], tw[:, 2 * u - 1 : 2 * u]
                         value, turned = cos * value - sin * turned, cos * turned + sin * value
-                    lanes_of = slice(128 * (u % 2), 128 * (u % 2) + 128)
-                    forward[u // 2, rows, lanes_of] = value.astype(BF16)
-                    forward[u // 2, low, lanes_of] = (-turned).astype(BF16)
-
+                    forward[u, rows, lanes_of] = value.astype(BF16)
+                    forward[u, low, lanes_of] = (-turned).astype(BF16)
+
+    def weigh(role, u, rows, spectrum):
+        weight = wd_dense[role, 0, u, rows, :].astype(F32)
+        return weight * (weight * spectrum - wd_dense[role, 1, u, rows, :].astype(F32))
+
+    def transform_columns():
+        for k in range(15):
+            y_copy(k).wait_recv()
         loop(4, fold_rows)
-        for pair in range(2):
+        for u in range(4):
+            for m in range(2):
+                rows = slice(256 * m, 256 * m + 256)
+                both = dot(fourier[rows, :], forward[u])
+                kept[0, u, rows, :] = weigh(0, u, rows, both[:, 0:128])
+                kept[1, u, rows, :] = both[:, 128:256]
+
+    def receive_swaps():
+        for copy in swaps:
+            copy.wait_recv()
+        for m in range(2):
+            rows = slice(256 * m, 256 * m + 256)
+            values = w_recv[rows, :]
+            turned = swap_halves(values)
+            left_lane = lanes((256, 128)) < 64
+            other_flat[256 * m : 256 * m + 256, :] = jnp.where(left_lane, values, turned)
+            other_flat[512 + 256 * m : 768 + 256 * m, :] = jnp.where(left_lane, turned, values)
+        rims = jnp.concatenate([rim_recv[...], jnp.zeros((120, 1024), F32)], axis=0).T.astype(BF16)
+        has_rim = me < 8
+        rim_w = one_hot((column_row == 0) & (half_lane == 0) & has_rim)
+        rim_d = one_hot((column_row == 1) & (lane_of == 0) & has_rim) - one_hot(
+            (column_row == 2) & (lane_of == 64) & has_rim
+        )
+        rim_flat[0] = dot(rims, rim_w)
+        rim_flat[1] = dot(rims, rim_d)
+        other_place, rim_place = place_of(ids_recv[0]), place_of(ids_recv[1])
+        for u in range(4):
+            put_dense(
+                1, u,
+                dot(other_place, by_row(other_flat, d_recv, u))
+                + dot(rim_place, by_row(rim_flat.at[0], rim_flat.at[1], u)),
+            )
+
+    def transform_back():
+        for u in range(4):
             for m in range(2):
                 rows, low = slice(256 * m, 256 * m + 256), slice(512 + 256 * m, 768 + 256 * m)
-                both = dot(fourier[rows, :], forward[pair])
-                for half in range(2):
-                    u = 2 * pair + half
-                    spectrum = both[:, 128 * half : 128 * half + 128]
-                    weight = wd_dense[0, e, u, rows, :].astype(F32)
-                    residual = weight * (weight * spectrum - wd_dense[1, e, u, rows, :].astype(F32))
-                    turned = times_i(residual).astype(BF16)
-                    residual = residual.astype(BF16)
-                    backward[u, rows, 0:128] = residual
-                    backward[u, low, 0:128] = turned
-                    if u > 0:
-                        backward[u, rows, 128:256] = turned
-                        backward[u, low, 128:256] = -residual
+                own, other = kept[0, u, rows, :], weigh(1, u, rows, kept[1, u, rows, :])
+                own_turned, other_swapped = times_i(own), swap_halves(other)
+                value = jnp.where(first_lane, own, jnp.where(middle_lane, other_swapped, own + other))
+                turned = jnp.where(
+                    first_lane, own_turned,
+                    jnp.where(middle_lane, other, own_turned - lane_sign * other_swapped),
+                )
+                value, turned = value.astype(BF16), turned.astype(BF16)
+                backward[u, rows, 0:128] = value
+                backward[u, low, 0:128] = turned
+                if u > 0:
+                    backward[u, rows, 128:256] = turned
+                    backward[u, low, 128:256] = -value
         for m in range(4):
             rows = slice(128 * m, 128 * m + 128)
             left_side = fourier[rows, :]
@@ -443,12 +490,28 @@
                     turned_odd = turned_odd - (cos * turned - sin * value)
             plus, minus, odd = terms[0] + terms[2], terms[0] - terms[2], terms[1] + terms[3]
             for j, value in enumerate((plus + odd, minus + turned_odd, plus - odd, minus - turned_odd)):
-                hsend[e, 512 * j + 128 * m : 512 * j + 128 * m + 128, :] = value
+                hsend[512 * j + 128 * m : 512 * j + 128 * m + 128, :] = value
         for k in range(15):
-            h_copy(e, k).start()
-        hrecv[e, me] = hsend[e, at(me, ROWS), :]
-
-    column_stage(0)
+            h_copy(k).start()
+        hrecv[me] = hsend[at(me, ROWS), :]
+
+    for bank in range(BANKS):
+        for copy in far_copies(bank):
+            copy.wait_recv()
+        low = pl.ds(pl.multiple_of(zp * QUARTER, QUARTER), 16)
+        high = pl.ds(pl.multiple_of(zm * QUARTER + 16, 16), 16)
+        squares[bank, low, :] = squares[bank, low, :] + far[bank, 0]
+        squares[bank, high, :] = squares[bank, high, :] + far[bank, 1]
+        for copy in near_copies(bank):
+            copy.start()
+    transform_columns()
+    for bank in range(BANKS):
+        for copy in near_copies(bank):
+            copy.wait_recv()
+        quarter_sum[bank] = squares[bank, at(z, QUARTER), :] + near[bank, 0] + near[bank, 1]
+        x_copy(bank).start()
+    swaps[5].start()
+
     bound = shrink_level * math.sqrt(8.0)
     for bank in range(BANKS):
         x_copy(bank).wait_recv()
@@ -456,7 +519,8 @@
         factor[bank, at(z, QUARTER), :] = bound / jnp.maximum(jnp.sqrt(total), bound)
         for copy in gather_near(bank):
             copy.start()
-    column_stage(1)
+    receive_swaps()
+    transform_back()
     for bank in range(BANKS):
         for copy in gather_near(bank):
             copy.wait_recv()
@@ -513,25 +577,14 @@
 
     loop(4, synthesise_columns)
 
-    for e in range(2):
-        for k in range(15):
-            h_copy(e, k).wait_recv()
-        for p in range(8):
-            value = hrecv[e, p]
-            if e == 1:
-                value = value + hrecv[e, 15 - p]
-            elif p == 0:
-                value = jnp.where(
-                    lane == 0, value,
-                    jnp.where(lane == 64, pltpu.roll(hrecv[0, 8], 64, 1), value + hrecv[0, 15]),
-                )
-            else:
-                value = value + jnp.where(edge_lane, hrecv[0, 16 - p], hrecv[0, 15 - p])
-            packed[e, :, 128 * p : 128 * p + 128] = value.astype(BF16)
+    for k in range(15):
+        h_copy(k).wait_recv()
+    for p in range(8):
+        packed[0, :, 128 * p : 128 * p + 128] = hrecv[p].astype(BF16)
+        packed[1, :, 128 * p : 128 * p + 128] = hrecv[15 - p].astype(BF16)
 
     def finish(i):
         cols = at(i, 256)
-        turn = (((1,), (1,)), ((), ()))
         even, odd = (
             lax.dot_general(packed[j], basis[j, cols, :], turn, preferred_element_type=F32)
             for j in range(2)
@@ -540,8 +593,8 @@
             (even + odd, cols),
             (even - odd, pl.ds(pl.multiple_of(1024 + i * 256, 256), 256)),
         ):
-            image_new[:, where] = jnp.maximum(
-                xpad[RIM : RIM + ROWS, where] - tau_primal * (gradient + adjoint[:, where]), 0.0
+            image_new[:, where] = xpad[RIM : RIM + ROWS, where] - tau_primal * (
+                gradient + adjoint[:, where]
             )
 
     loop(4, finish)
@@ -550,10 +603,11 @@
 
     for copy in halos:
         copy.wait_send()
-    for e in range(2):
-        for k in range(15):
-            y_copy(e, k).wait_send()
-            h_copy(e, k).wait_send()
+    for k in range(15):
+        y_copy(k).wait_send()
+        h_copy(k).wait_send()
+    for copy in swaps:
+        copy.wait_send()
     for bank in range(BANKS):
         for copy in far_copies(bank) + near_copies(bank) + gather_near(bank) + gather_far(bank):
             copy.wait_send()
@@ -574,8 +628,30 @@
     ]
 
 
+def clip_kernel(image_hbm, dual_hbm, image_out, dual_out, image, dual, in_sem, out_sem):
+    parts = [
+        (image_hbm.at[32 * i : 32 * i + 32], image.at[32 * i : 32 * i + 32], image_out.at[32 * i : 32 * i + 32])
+        for i in range(4)
+    ] + [
+        (dual_hbm.at[b, 64 * i : 64 * i + 64], dual.at[b, 64 * i : 64 * i + 64], dual_out.at[b, 64 * i : 64 * i + 64])
+        for b in range(2)
+        for i in range(2)
+    ]
+    reads = [pltpu.make_async_copy(p[0], p[1], in_sem.at[i]) for i, p in enumerate(parts)]
+    writes = [pltpu.make_async_copy(p[1], p[2], out_sem.at[i]) for i, p in enumerate(parts)]
+    for read in reads:
+        read.start()
+    for i, (read, write) in enumerate(zip(reads, writes)):
+        read.wait()
+        if i < 4:
+            image[32 * i : 32 * i + 32] = jnp.maximum(image[32 * i : 32 * i + 32], 0.0)
+        write.start()
+    for write in writes:
+        write.wait()
+
+
 def per_device(constants, image, dual_coeffs, block_ids, block_counts, block_weights, block_data):
-    any_space = pl.BlockSpec(memory_space=pl.ANY)
+    any_space = in_hbm = pl.BlockSpec(memory_space=pl.ANY)
     in_vmem = pl.BlockSpec(memory_space=pltpu.VMEM)
     dma = lambda *n: pltpu.SemaphoreType.DMA(n)
     vmem = pltpu.VMEM
@@ -602,10 +678,10 @@
             vmem((768, 128), BF16),
             vmem((2, 1024, 1024), BF16),
             vmem((2, ROWS, 1024), BF16),
-            vmem((2, STRIPS, ROWS, 128), F32),
-            vmem((2, PIX, 128), F32),
-            vmem((2, PIX, 128), F32),
-            vmem((2, STRIPS, ROWS, 128), F32),
+            vmem((STRIPS, ROWS, 128), F32),
+            vmem((PIX, 128), F32),
+            vmem((PIX, 128), F32),
+            vmem((STRIPS, ROWS, 128), F32),
             vmem((BANKS, PAD, PIX), BF16),
             vmem((BANKS, ROWS, PIX), F32),
             vmem((BANKS, ROWS, PIX), F32),
@@ -619,15 +695,26 @@
             vmem((BANKS, 2, RIM, PIX), F32),
             vmem((BANKS, ROWS, PIX + 256), BF16),
             vmem((ROWS, PIX), F32),
-            vmem((4, 1024, 128), F32),
+            vmem((2, 1024, 128), F32),
+            vmem((1024, 128), F32),
+            vmem((2, 1024, 128), F32),
+            vmem((512, 128), F32),
+            vmem((512, 128), F32),
+            vmem((1024, 128), F32),
+            vmem((1024, 128), F32),
+            vmem((8, 256), F32),
+            vmem((2, 8, 256), F32),
+            vmem((8, 1024), F32),
+            vmem((8, 1024), F32),
             vmem((2, 2, 4, 512, 128), BF16),
-            vmem((2, 1024, 256), BF16),
+            vmem((4, 1024, 256), BF16),
+            vmem((2, 4, 512, 128), F32),
             vmem((4, 1024, 256), BF16),
             vmem((2, ROWS, 1024), BF16),
             vmem((ROWS, PIX), F32),
             vmem((BANKS, ROWS, PIX), BF16),
-            dma(11), dma(2, 15), dma(2, 15), dma(2, 15), dma(2, 15), dma(2), dma(2), dma(4), dma(4),
-            dma(4), dma(4), dma(4), dma(4), dma(2), dma(2), dma(4), dma(4), dma(4), dma(4), dma(2),
+            dma(11), dma(15), dma(15), dma(15), dma(15), dma(2), dma(2), dma(4), dma(4),
+            dma(4), dma(4), dma(4), dma(4), dma(2), dma(2), dma(4), dma(4), dma(4), dma(4), dma(6), dma(6), dma(2),
         ],
         compiler_params=pltpu.CompilerParams(
             collective_id=0, has_side_effects=True, vmem_limit_bytes=60 * 1024 * 1024
@@ -641,6 +728,17 @@
         block_data[0],
         *constants,
     )
+    image_new, dual_new = pl.pallas_call(
+        clip_kernel,
+        out_shape=(
+            jax.ShapeDtypeStruct((ROWS, PIX), F32),
+            jax.ShapeDtypeStruct((BANKS, ROWS, PIX), BF16),
+        ),
+        in_specs=[in_hbm, in_hbm],
+        out_specs=(in_hbm, in_hbm),
+        scratch_shapes=[vmem((ROWS, PIX), F32), vmem((BANKS, ROWS, PIX), BF16), dma(8), dma(8)],
+        compiler_params=pltpu.CompilerParams(vmem_limit_bytes=60 * 1024 * 1024),
+    )(image_new, dual_new)
     return image_new[None], dual_new[:, None]
 
 

time: 81.1 us -> 81.2 us (level)
  Pallas kernels: 76.3 us -> 79.8 us
  local copies, waits for them, and re-layouts: 3.36 us -> 0 us
    unnamed x4 -> x0, local copies, waits for them, and re-layouts: 3.36 us -> none
    pallas_call x0 -> x1, Pallas kernels: none -> 2.41 us  [per_device(): pl.pallas_call(clip_kernel, out_shape=(jax.ShapeDtypeStruct((ROWS, PIX),...]
    pallas_call x1, Pallas kernels: 76.3 us -> 77.4 us  [per_device(): pl.pallas_call(kernel, out_shape=(jax.ShapeDtypeStruct((ROWS, PIX), F32),...]
where the time goes in v2:
time: 81.2 us; the launch traced here: 81.1 us
  Pallas kernels  79.8 us (98%)
  between operations  1.28 us (2%)
    pallas_call x1, Pallas kernels, per_device(): pl.pallas_call(kernel, out_shape=(jax.ShapeDtypeStruct((ROWS, PIX), F32),...  77.4 us
    pallas_call x1, Pallas kernels, per_device(): pl.pallas_call(clip_kernel, out_shape=(jax.ShapeDtypeStruct((ROWS, PIX),...  2.41 us

profile of v2, /device:TPU:0, one launch (start us, length us, event | category | flops | bytes accessed | tf_op | source)
XLA Modules:
  0.0 81.1 jit_solution(9387882044780903728)
XLA Ops:
  1.3 77.4 %shard_map.140 = (f32[128,2048]{1,0:T(8,128)}, bf16[2,128,2048]{2,1,0:T(8,128)(2,1)}) custom-call(f32[128,2048]{1,0:T(8,128)} %bitcast.8, bf16[2,128,2048]{2,1,0:T(8,128)(2,1)} %bitcast.9, s32[1,32]{1,0:T(1,128)} %ids_ref.1, s32[1,1]{1,0:T(1,128)S(6)} %copy.16.counts_ref, bf16[32,32,128]{2,1,0:T(8,128)(2,1)} %bitcast.11, bf16[2,32,32,128]{3,2,1,0:T(8,128)(2,1)} %bitcast.10, ...), custom_call_target="tpu_custom_call" | custom-call | tf_op jit(solution)/shard_map/pallas_call | solution.py:658
  78.7 2.4 %shard_map.141 = (f32[128,2048]{1,0:T(8,128)}, bf16[2,128,2048]{2,1,0:T(8,128)(2,1)}) custom-call(f32[128,2048]{1,0:T(8,128)} %get-tuple-element.6.image_hbm, bf16[2,128,2048]{2,1,0:T(8,128)(2,1)} %get-tuple-element.7.dual_hbm), custom_call_target="tpu_custom_call" | custom-call | tf_op jit(solution)/shard_map/pallas_call | solution.py:731

commit v3 on v2

--- a/solution.py
+++ b/solution.py
@@ -18,6 +18,7 @@
 PAD = ROWS + 2 * RIM
 BANKS = 2
 QUARTER = ROWS // 4
+CHUNKS = 4
 FAR_FIRST = [
     (dx, dy, core)
     for dx, dy in ((1, 2), (0, 2), (1, 1), (1, 3), (0, 1), (0, 3), (1, 0))
@@ -90,7 +91,10 @@
         [bank_matrix(t, 128, 128, 0, 384).T for t in bank_filters], axis=1
     )
     ana_rows = np.stack([sigma_dual * bank_matrix(t, RIM, ROWS, 0, PAD) for t in bank_filters])
-    syn_rows = np.stack([bank_matrix(t, 0, PAD, RIM, ROWS).T for t in bank_filters])
+    syn_all = np.stack([bank_matrix(t, 0, PAD, RIM, ROWS).T for t in bank_filters])
+    syn_rows = syn_all[:, :, RIM : RIM + ROWS]
+    rims = np.concatenate([syn_all[:, :, 0:RIM], syn_all[:, :, RIM + ROWS :]], axis=2)
+    syn_rims = np.concatenate([rims[:, 0:16], rims[:, ROWS - 16 :]], axis=1)
     syn_cols = np.concatenate([bank_matrix(t, 0, 384, 128, 128) for t in bank_filters], axis=0)
     as_bf16 = lambda a: np.asarray(a, np.float32).astype(BF16)
     return (
@@ -100,6 +104,7 @@
         as_bf16(ana_cols),
         as_bf16(ana_rows),
         as_bf16(syn_rows),
+        as_bf16(syn_rims),
         as_bf16(syn_cols),
     )
 
@@ -131,9 +136,9 @@
 
 def kernel(
     image_hbm, dual_hbm, ids_ref, counts_ref, weights_hbm, data_hbm,
-    tables_hbm, fourier_hbm, twiddle_hbm, ana_cols_hbm, ana_rows_hbm, syn_rows_hbm, syn_cols_hbm,
+    tables_hbm, fourier_hbm, twiddle_hbm, ana_cols_hbm, ana_rows_hbm, syn_rows_hbm, syn_rims_hbm, syn_cols_hbm,
     image_out, dual_out,
-    xpad, xwide, dual, weights, data, tables, fourier, twiddle, ana_cols, ana_rows, syn_rows, syn_cols,
+    xpad, xwide, dual, weights, data, tables, fourier, twiddle, ana_cols, ana_rows, syn_rows, syn_rims, syn_cols,
     basis, folded, ysend, yrecv, hsend, hrecv, coeffs, trial, squares, near, far, quarter_sum, other_sum,
     factor, combined, edge_send, edge_recv, synth_wide, adjoint, own_flat, other_flat, rim_flat,
     w_send, w_recv, d_send, d_recv, ids_send, ids_recv, rim_send, rim_recv, wd_dense,
@@ -152,25 +157,25 @@
     before, after = {"strip": (me + 15) % STRIPS}, {"strip": (me + 1) % STRIPS}
     sign = jnp.where(me < 8, 1, -1)
 
-    loads = [
-        pltpu.make_async_copy(src, dst, local_sem.at[i])
-        for i, (src, dst) in enumerate(
-            [
-                (tables_hbm, tables),
-                (image_hbm, xpad.at[RIM : RIM + ROWS]),
-                (ana_cols_hbm, ana_cols),
-                (ana_rows_hbm, ana_rows),
-                (dual_hbm, dual),
-                (weights_hbm, weights),
-                (data_hbm, data),
-                (fourier_hbm, fourier),
-                (twiddle_hbm, twiddle),
-                (syn_rows_hbm, syn_rows),
-                (syn_cols_hbm, syn_cols),
-            ]
-        )
-    ]
-    for load in loads:
+    sources = {
+        "weights": (weights_hbm, weights),
+        "data": (data_hbm, data),
+        "image": (image_hbm, xpad.at[RIM : RIM + ROWS]),
+        "tables": (tables_hbm, tables),
+        "ana_cols": (ana_cols_hbm, ana_cols),
+        "ana_rows": (ana_rows_hbm, ana_rows),
+        "dual": (dual_hbm, dual),
+        "fourier": (fourier_hbm, fourier),
+        "twiddle": (twiddle_hbm, twiddle),
+        "syn_rows": (syn_rows_hbm, syn_rows),
+        "syn_rims": (syn_rims_hbm, syn_rims),
+        "syn_cols": (syn_cols_hbm, syn_cols),
+    }
+    loads = {
+        name: pltpu.make_async_copy(src, dst, local_sem.at[i])
+        for i, (name, (src, dst)) in enumerate(sources.items())
+    }
+    for load in loads.values():
         load.start()
 
     barrier = pltpu.get_barrier_semaphore()
@@ -180,121 +185,13 @@
         )
     for peer in (up, down, across):
         pl.semaphore_signal(barrier, inc=1, device_id=peer, device_id_type=MESH)
-    pl.semaphore_wait(barrier, STRIPS + 2)
-
     def remote(src, dst, send, recv, peer):
         return pltpu.make_async_remote_copy(
             src_ref=src, dst_ref=dst, send_sem=send, recv_sem=recv, device_id=peer, device_id_type=MESH
         )
 
-    halos = [
-        remote(xpad.at[RIM : 2 * RIM], xpad.at[RIM + ROWS : PAD], halo_s.at[0], halo_r.at[0], before),
-        remote(xpad.at[ROWS : RIM + ROWS], xpad.at[0:RIM], halo_s.at[1], halo_r.at[1], after),
-    ]
-    loads[0].wait()
-    for parity in range(2):
-        def make_basis(i, parity=parity):
-            coarse_cos = tables[4 * parity, pl.ds(i, 1), :]
-            coarse_sin = tables[4 * parity + 1, pl.ds(i, 1), :]
-            block = coarse_cos * tables[4 * parity + 2] - coarse_sin * tables[4 * parity + 3]
-            basis[parity, at(i, 32), :] = block.astype(BF16)
-
-        loop(32, make_basis)
-    loads[1].wait()
-    for copy in halos:
-        copy.start()
-    left, right = xpad[RIM : RIM + ROWS, 0:1024], xpad[RIM : RIM + ROWS, 1024:2048]
-    folded[0] = (left + right).astype(BF16)
-    folded[1] = (left - right).astype(BF16)
-    def y_copy(k):
-        q = peer_at(me, k)
-        return remote(ysend.at[q], yrecv.at[at(me, ROWS)], y_s.at[k], y_r.at[k], {"strip": q})
-
-    for e in range(2):
-        for pair in range(4):
-            tiles = dot(folded[e], basis[e, :, 256 * pair : 256 * pair + 256])
-            for half in range(2):
-                p = 2 * pair + half
-                ysend[15 - p if e else p] = tiles[:, 128 * half : 128 * half + 128]
-    for k in range(15):
-        y_copy(k).start()
-    yrecv[at(me, ROWS), :] = ysend[me]
-
-    for copy in halos:
-        copy.wait_recv()
-    for i in (2, 3, 4):
-        loads[i].wait()
-    xwide[:, 0:128] = jnp.zeros((PAD, 128), BF16)
-    xwide[:, 128 + PIX : 256 + PIX] = jnp.zeros((PAD, 128), BF16)
-    row = lax.broadcasted_iota(jnp.int32, (PAD, PIX), 0)
-    outside = ((row < RIM) & (me == 0)) | ((row >= RIM + ROWS) & (me == STRIPS - 1))
-    xwide[:, 128 : 128 + PIX] = jnp.where(outside, 0.0, xpad[...]).astype(BF16)
-
-    def analyse_columns(i):
-        for t in range(4):
-            start = pl.multiple_of(i * 512 + t * 128, 128)
-            both = dot(xwide[:, pl.ds(start, 384)], ana_cols[...]).astype(BF16)
-            coeffs[0, :, pl.ds(start, 128)] = both[:, 0:128]
-            coeffs[1, :, pl.ds(start, 128)] = both[:, 128:256]
-
-    loop(4, analyse_columns)
-
-    def far_copies(bank):
-        return [
-            remote(
-                squares.at[bank, pl.ds(pl.multiple_of(zf * QUARTER, QUARTER), 16)],
-                far.at[bank, 0], far_s.at[2 * bank], far_r.at[2 * bank], up,
-            ),
-            remote(
-                squares.at[bank, pl.ds(pl.multiple_of(zf * QUARTER + 16, 16), 16)],
-                far.at[bank, 1], far_s.at[2 * bank + 1], far_r.at[2 * bank + 1], down,
-            ),
-        ]
-
-    def near_copies(bank):
-        return [
-            remote(
-                squares.at[bank, at(zp, QUARTER)], near.at[bank, 0],
-                near_s.at[2 * bank], near_r.at[2 * bank], up,
-            ),
-            remote(
-                squares.at[bank, at(zm, QUARTER)], near.at[bank, 1],
-                near_s.at[2 * bank + 1], near_r.at[2 * bank + 1], down,
-            ),
-        ]
-
-    def x_copy(bank):
-        return remote(quarter_sum.at[bank], other_sum.at[bank], x_s.at[bank], x_r.at[bank], across)
-
-    def gather_near(bank):
-        mine = factor.at[bank, at(z, QUARTER)]
-        return [
-            remote(mine, mine, ga_s.at[2 * bank], ga_r.at[2 * bank], up),
-            remote(mine, mine, ga_s.at[2 * bank + 1], ga_r.at[2 * bank + 1], down),
-        ]
-
-    def gather_far(bank):
-        low = factor.at[bank, pl.ds(pl.multiple_of(zm * QUARTER, QUARTER), 16)]
-        high = factor.at[bank, pl.ds(pl.multiple_of(zp * QUARTER + 16, 16), 16)]
-        return [
-            remote(low, low, gb_s.at[2 * bank], gb_r.at[2 * bank], up),
-            remote(high, high, gb_s.at[2 * bank + 1], gb_r.at[2 * bank + 1], down),
-        ]
-
-    for bank in range(BANKS):
-        def analyse_rows(i, bank=bank):
-            for t in range(4):
-                cols = pl.ds(pl.multiple_of(i * 1024 + t * 256, 256), 256)
-                values = dual[bank, :, cols].astype(F32) + dot(ana_rows[bank], coeffs[bank, :, cols])
-                trial[bank, :, cols] = values
-                squares[bank, :, cols] = values * values
-
-        loop(2, analyse_rows)
-        for copy in far_copies(bank):
-            copy.start()
-
-    for i in (5, 6, 7, 8):
-        loads[i].wait()
+    loads["weights"].wait()
+    loads["data"].wait()
     lane_of = lanes((128, 128))
     half_lane = lane_of % 64
     imag_lane = lane_of >= 64
@@ -335,16 +232,132 @@
         select = one_hot((sel_row == i) & (sel_lane == 0))
         rim = rim + lax.dot_general(select, values.reshape(1024, 128), turn, preferred_element_type=F32)
     rim_send[...] = rim
+    pl.semaphore_wait(barrier, STRIPS + 2)
+
+    halos = [
+        remote(xpad.at[RIM : 2 * RIM], xpad.at[RIM + ROWS : PAD], halo_s.at[0], halo_r.at[0], before),
+        remote(xpad.at[ROWS : RIM + ROWS], xpad.at[0:RIM], halo_s.at[1], halo_r.at[1], after),
+    ]
+    loads["image"].wait()
+    for copy in halos:
+        copy.start()
     swaps = [
         remote(w_send, w_recv, swap_s.at[0], swap_r.at[0], mirror),
         remote(ids_send, ids_recv.at[0], swap_s.at[1], swap_r.at[1], mirror),
         remote(ids_send, ids_recv.at[1], swap_s.at[2], swap_r.at[2], rim_peer),
         remote(rim_send, rim_recv, swap_s.at[3], swap_r.at[3], rim_peer),
-        remote(d_send.at[0:512], d_recv.at[0:512], swap_s.at[4], swap_r.at[4], mirror),
-        remote(d_send.at[512:1024], d_recv.at[512:1024], swap_s.at[5], swap_r.at[5], mirror),
+        remote(d_send, d_recv, swap_s.at[4], swap_r.at[4], mirror),
     ]
-    for copy in swaps[0:5]:
+    for copy in swaps:
         copy.start()
+
+    loads["tables"].wait()
+    for parity in range(2):
+        def make_basis(i, parity=parity):
+            coarse_cos = tables[4 * parity, pl.ds(i, 1), :]
+            coarse_sin = tables[4 * parity + 1, pl.ds(i, 1), :]
+            block = coarse_cos * tables[4 * parity + 2] - coarse_sin * tables[4 * parity + 3]
+            basis[parity, at(i, 32), :] = block.astype(BF16)
+
+        loop(32, make_basis)
+    left, right = xpad[RIM : RIM + ROWS, 0:1024], xpad[RIM : RIM + ROWS, 1024:2048]
+    folded[0] = (left + right).astype(BF16)
+    folded[1] = (left - right).astype(BF16)
+    def y_copy(k):
+        q = peer_at(me, k)
+        return remote(ysend.at[q], yrecv.at[at(me, ROWS)], y_s.at[k], y_r.at[k], {"strip": q})
+
+    for e in range(2):
+        for pair in range(4):
+            tiles = dot(folded[e], basis[e, :, 256 * pair : 256 * pair + 256])
+            for half in range(2):
+                p = 2 * pair + half
+                ysend[15 - p if e else p] = tiles[:, 128 * half : 128 * half + 128]
+    for k in range(15):
+        y_copy(k).start()
+    yrecv[at(me, ROWS), :] = ysend[me]
+
+    for copy in halos:
+        copy.wait_recv()
+    for name in ("ana_cols", "ana_rows", "dual"):
+        loads[name].wait()
+    xwide[:, 0:128] = jnp.zeros((PAD, 128), BF16)
+    xwide[:, 128 + PIX : 256 + PIX] = jnp.zeros((PAD, 128), BF16)
+    row = lax.broadcasted_iota(jnp.int32, (PAD, PIX), 0)
+    outside = ((row < RIM) & (me == 0)) | ((row >= RIM + ROWS) & (me == STRIPS - 1))
+    xwide[:, 128 : 128 + PIX] = jnp.where(outside, 0.0, xpad[...]).astype(BF16)
+
+    def analyse_columns(i):
+        for t in range(4):
+            start = pl.multiple_of(i * 512 + t * 128, 128)
+            both = dot(xwide[:, pl.ds(start, 384)], ana_cols[...]).astype(BF16)
+            coeffs[0, :, pl.ds(start, 128)] = both[:, 0:128]
+            coeffs[1, :, pl.ds(start, 128)] = both[:, 128:256]
+
+    loop(4, analyse_columns)
+
+    def cols_of(c):
+        return slice(1024 * (c % 2), 1024 * (c % 2) + 1024)
+
+    def far_copies(c):
+        bank, cols = c // 2, cols_of(c)
+        low = pl.ds(pl.multiple_of(zf * QUARTER, QUARTER), 16)
+        high = pl.ds(pl.multiple_of(zf * QUARTER + 16, 16), 16)
+        return [
+            remote(squares.at[bank, low, cols], far.at[bank, 0, :, cols], far_s.at[c, 0], far_r.at[c, 0], up),
+            remote(squares.at[bank, high, cols], far.at[bank, 1, :, cols], far_s.at[c, 1], far_r.at[c, 1], down),
+        ]
+
+    def near_copies(c):
+        bank, cols = c // 2, cols_of(c)
+        return [
+            remote(
+                squares.at[bank, at(where, QUARTER), cols], near.at[bank, side, :, cols],
+                near_s.at[c, side], near_r.at[c, side], peer,
+            )
+            for side, (where, peer) in enumerate(((zp, up), (zm, down)))
+        ]
+
+    def x_copy(c):
+        bank, cols = c // 2, cols_of(c)
+        return remote(
+            quarter_sum.at[bank, :, cols], other_sum.at[bank, :, cols], x_s.at[c], x_r.at[c], across
+        )
+
+    def gather_near(c):
+        mine = factor.at[c // 2, at(z, QUARTER), cols_of(c)]
+        return [
+            remote(mine, mine, ga_s.at[c, side], ga_r.at[c, side], peer)
+            for side, peer in enumerate((up, down))
+        ]
+
+    def gather_far(c):
+        low = factor.at[c // 2, pl.ds(pl.multiple_of(zm * QUARTER, QUARTER), 16), cols_of(c)]
+        high = factor.at[c // 2, pl.ds(pl.multiple_of(zp * QUARTER + 16, 16), 16), cols_of(c)]
+        return [
+            remote(low, low, gb_s.at[c, 0], gb_r.at[c, 0], up),
+            remote(high, high, gb_s.at[c, 1], gb_r.at[c, 1], down),
+        ]
+
+    def edge_copies(c):
+        cols = cols_of(c)
+        return [
+            remote(
+                edge_send.at[c // 2, side, :, cols], edge_recv.at[c // 2, side, :, cols],
+                edge_s.at[c, side], edge_r.at[c, side], peer,
+            )
+            for side, peer in enumerate((before, after))
+        ]
+
+    for c in range(CHUNKS):
+        bank = c // 2
+        for t in range(4):
+            cols = slice(1024 * (c % 2) + 256 * t, 1024 * (c % 2) + 256 * t + 256)
+            values = dual[bank, :, cols].astype(F32) + dot(ana_rows[bank], coeffs[bank, :, cols])
+            trial[bank, :, cols] = values
+            squares[bank, :, cols] = values * values
+        for copy in far_copies(c):
+            copy.start()
 
     for i in range(4):
         rows = slice(256 * i, 256 * i + 256)
@@ -495,87 +508,123 @@
             h_copy(k).start()
         hrecv[me] = hsend[at(me, ROWS), :]
 
-    for bank in range(BANKS):
-        for copy in far_copies(bank):
+    def send_near(c):
+        bank, cols = c // 2, cols_of(c)
+        for copy in far_copies(c):
             copy.wait_recv()
         low = pl.ds(pl.multiple_of(zp * QUARTER, QUARTER), 16)
         high = pl.ds(pl.multiple_of(zm * QUARTER + 16, 16), 16)
-        squares[bank, low, :] = squares[bank, low, :] + far[bank, 0]
-        squares[bank, high, :] = squares[bank, high, :] + far[bank, 1]
-        for copy in near_copies(bank):
+        squares[bank, low, cols] = squares[bank, low, cols] + far[bank, 0, :, cols]
+        squares[bank, high, cols] = squares[bank, high, cols] + far[bank, 1, :, cols]
+        for copy in near_copies(c):
             copy.start()
-    transform_columns()
-    for bank in range(BANKS):
-        for copy in near_copies(bank):
+
+    def send_across(c):
+        bank, cols = c // 2, cols_of(c)
+        for copy in near_copies(c):
             copy.wait_recv()
-        quarter_sum[bank] = squares[bank, at(z, QUARTER), :] + near[bank, 0] + near[bank, 1]
-        x_copy(bank).start()
-    swaps[5].start()
+        quarter_sum[bank, :, cols] = (
+            squares[bank, at(z, QUARTER), cols] + near[bank, 0, :, cols] + near[bank, 1, :, cols]
+        )
+        x_copy(c).start()
 
     bound = shrink_level * math.sqrt(8.0)
-    for bank in range(BANKS):
-        x_copy(bank).wait_recv()
-        total = quarter_sum[bank] + other_sum[bank]
-        factor[bank, at(z, QUARTER), :] = bound / jnp.maximum(jnp.sqrt(total), bound)
-        for copy in gather_near(bank):
+
+    def send_factor(c):
+        bank, cols = c // 2, cols_of(c)
+        x_copy(c).wait_recv()
+        total = quarter_sum[bank, :, cols] + other_sum[bank, :, cols]
+        factor[bank, at(z, QUARTER), cols] = bound / jnp.maximum(jnp.sqrt(total), bound)
+        for copy in gather_near(c):
             copy.start()
-    receive_swaps()
-    transform_back()
-    for bank in range(BANKS):
-        for copy in gather_near(bank):
+
+    def pass_factor(c):
+        for copy in gather_near(c):
             copy.wait_recv()
-        for copy in gather_far(bank):
+        for copy in gather_far(c):
             copy.start()
 
-    dual_outs = []
-    for bank in range(BANKS):
-        for copy in gather_far(bank):
+    def shrink(c):
+        bank, cols = c // 2, cols_of(c)
+        for copy in gather_far(c):
             copy.wait_recv()
-
-        def shrink(i, bank=bank):
-            rows = at(i, 16)
-            fresh = (trial[bank, rows, :] * factor[bank, rows, :]).astype(BF16)
-            dual_new[bank, rows, :] = fresh
-            inner = pl.ds(pl.multiple_of(RIM + i * 16, 8), 16)
-            combined[bank, inner, :] = 2.0 * fresh.astype(F32) - dual[bank, rows, :].astype(F32)
-
-        loop(8, shrink)
-        edge_send[bank, 0] = combined[bank, RIM : 2 * RIM]
-        edge_send[bank, 1] = combined[bank, ROWS : RIM + ROWS]
-        for copy in edge_copies(remote, bank, edge_send, edge_recv, edge_s, edge_r, before, after):
+        for i in range(8):
+            rows = slice(16 * i, 16 * i + 16)
+            fresh = (trial[bank, rows, cols] * factor[bank, rows, cols]).astype(BF16)
+            dual_new[bank, rows, cols] = fresh
+            values = 2.0 * fresh.astype(F32) - dual[bank, rows, cols].astype(F32)
+            combined[bank, rows, cols] = values.astype(BF16)
+            if i == 0:
+                edge_send[bank, 0, :, cols] = values[0:RIM]
+            if i == 7:
+                edge_send[bank, 1, :, cols] = values[16 - RIM : 16]
+        for copy in edge_copies(c):
             copy.start()
-    dual_copy = pltpu.make_async_copy(dual_new, dual_out, out_sem.at[0])
-    dual_copy.start()
-
-    for bank in range(BANKS):
-        for copy in edge_copies(remote, bank, edge_send, edge_recv, edge_s, edge_r, before, after):
+
+    def synthesise_rows(c):
+        bank = c // 2
+        for t in range(4):
+            start = 1024 * (c % 2) + 256 * t
+            values = dot(syn_rows[bank], combined[bank, :, start : start + 256])
+            synth_wide[bank, :, 128 + start : 384 + start] = values.astype(BF16)
+
+    def add_edges(c):
+        bank, cols = c // 2, cols_of(c)
+        wide = slice(128 + 1024 * (c % 2), 1152 + 1024 * (c % 2))
+        for copy in edge_copies(c):
             copy.wait_recv()
-        combined[bank, RIM + ROWS : PAD] = jnp.where(me == STRIPS - 1, 0.0, edge_recv[bank, 0])
-        combined[bank, 0:RIM] = jnp.where(me == 0, 0.0, edge_recv[bank, 1])
-    for i in (9, 10):
-        loads[i].wait()
+        below = jnp.where(me == STRIPS - 1, 0.0, edge_recv[bank, 0, :, cols])
+        above = jnp.where(me == 0, 0.0, edge_recv[bank, 1, :, cols])
+        extra = dot(syn_rims[bank], jnp.concatenate([above, below], axis=0).astype(BF16))
+        for rows, part in ((slice(0, 16), extra[0:16]), (slice(ROWS - 16, ROWS), extra[16:32])):
+            synth_wide[bank, rows, wide] = (synth_wide[bank, rows, wide].astype(F32) + part).astype(BF16)
+
+    def synthesise_columns(i, rows):
+        for t in range(4):
+            start = pl.multiple_of(i * 512 + t * 128, 128)
+            window = pl.ds(start, 384)
+            adjoint[rows, pl.ds(start, 128)] = dot(synth_wide[0, rows, window], syn_cols[0:384]) + dot(
+                synth_wide[1, rows, window], syn_cols[384:768]
+            )
+
+    inner, outer = slice(16, ROWS - 16), (slice(0, 16), slice(ROWS - 16, ROWS))
+
+    for c in range(CHUNKS):
+        send_near(c)
+    for name in ("fourier", "twiddle", "syn_rows", "syn_rims", "syn_cols"):
+        loads[name].wait()
     for bank in range(BANKS):
         synth_wide[bank, :, 0:128] = jnp.zeros((ROWS, 128), BF16)
         synth_wide[bank, :, 128 + PIX : 256 + PIX] = jnp.zeros((ROWS, 128), BF16)
-
-        def synthesise_rows(i, bank=bank):
-            for t in range(4):
-                start = i * 1024 + t * 256
-                cols = pl.ds(pl.multiple_of(start, 256), 256)
-                values = dot(syn_rows[bank], combined[bank, :, cols].astype(BF16))
-                synth_wide[bank, :, pl.ds(pl.multiple_of(128 + start, 128), 256)] = values.astype(BF16)
-
-        loop(2, synthesise_rows)
-
-    def synthesise_columns(i):
-        for t in range(4):
-            start = pl.multiple_of(i * 512 + t * 128, 128)
-            window = pl.ds(start, 384)
-            adjoint[:, pl.ds(start, 128)] = dot(synth_wide[0, :, window], syn_cols[0:384]) + dot(
-                synth_wide[1, :, window], syn_cols[384:768]
-            )
-
-    loop(4, synthesise_columns)
+    send_across(0)
+    send_across(1)
+    send_across(2)
+    send_across(3)
+    transform_columns()
+    send_factor(0)
+    send_factor(1)
+    send_factor(2)
+    receive_swaps()
+    transform_back()
+    send_factor(3)
+    pass_factor(0)
+    pass_factor(1)
+    pass_factor(2)
+    pass_factor(3)
+    shrink(0)
+    synthesise_rows(0)
+    shrink(1)
+    synthesise_rows(1)
+    shrink(2)
+    synthesise_rows(2)
+    shrink(3)
+    synthesise_rows(3)
+    dual_copy = pltpu.make_async_copy(dual_new, dual_out, out_sem.at[0])
+    dual_copy.start()
+    loop(4, lambda i: synthesise_columns(i, inner))
+    for c in range(CHUNKS):
+        add_edges(c)
+    loop(4, lambda i: [synthesise_columns(i, rows) for rows in outer])
 
     for k in range(15):
         h_copy(k).wait_recv()
@@ -597,9 +646,20 @@
                 gradient + adjoint[:, where]
             )
 
-    loop(4, finish)
-    image_copy = pltpu.make_async_copy(image_new, image_out, out_sem.at[1])
-    image_copy.start()
+    def image_copies(i):
+        return [
+            pltpu.make_async_copy(image_new.at[:, cols], image_out.at[:, cols], out_sem.at[1 + 2 * i + side])
+            for side, cols in enumerate(
+                (at(i, 256), pl.ds(pl.multiple_of(1024 + i * 256, 256), 256))
+            )
+        ]
+
+    def finish_and_send(i):
+        finish(i)
+        for copy in image_copies(i):
+            copy.start()
+
+    loop(4, finish_and_send)
 
     for copy in halos:
         copy.wait_send()
@@ -608,24 +668,14 @@
         h_copy(k).wait_send()
     for copy in swaps:
         copy.wait_send()
-    for bank in range(BANKS):
-        for copy in far_copies(bank) + near_copies(bank) + gather_near(bank) + gather_far(bank):
+    for c in range(CHUNKS):
+        for copy in far_copies(c) + near_copies(c) + gather_near(c) + gather_far(c) + edge_copies(c):
             copy.wait_send()
-        x_copy(bank).wait_send()
-        for copy in edge_copies(remote, bank, edge_send, edge_recv, edge_s, edge_r, before, after):
-            copy.wait_send()
+        x_copy(c).wait_send()
     dual_copy.wait()
-    image_copy.wait()
-
-
-def edge_copies(remote, bank, edge_send, edge_recv, edge_s, edge_r, before, after):
-    return [
-        remote(
-            edge_send.at[bank, side], edge_recv.at[bank, side],
-            edge_s.at[2 * bank + side], edge_r.at[2 * bank + side], (before, after)[side],
-        )
-        for side in range(2)
-    ]
+    for i in range(4):
+        for copy in image_copies(i):
+            copy.wait()
 
 
 def clip_kernel(image_hbm, dual_hbm, image_out, dual_out, image, dual, in_sem, out_sem):
@@ -661,7 +711,7 @@
             jax.ShapeDtypeStruct((ROWS, PIX), F32),
             jax.ShapeDtypeStruct((BANKS, ROWS, PIX), BF16),
         ),
-        in_specs=[any_space, any_space, in_vmem, in_vmem] + [any_space] * 9,
+        in_specs=[any_space, any_space, in_vmem, in_vmem] + [any_space] * 10,
         out_specs=(any_space, any_space),
         scratch_shapes=[
             vmem((PAD, PIX), F32),
@@ -674,7 +724,8 @@
             vmem((512, 128), F32),
             vmem((384, 256), BF16),
             vmem((BANKS, ROWS, PAD), BF16),
-            vmem((BANKS, ROWS, PAD), BF16),
+            vmem((BANKS, ROWS, ROWS), BF16),
+            vmem((BANKS, 32, 2 * RIM), BF16),
             vmem((768, 128), BF16),
             vmem((2, 1024, 1024), BF16),
             vmem((2, ROWS, 1024), BF16),
@@ -690,7 +741,7 @@
             vmem((BANKS, QUARTER, PIX), F32),
             vmem((BANKS, QUARTER, PIX), F32),
             vmem((BANKS, ROWS, PIX), F32),
-            vmem((BANKS, PAD, PIX), F32),
+            vmem((BANKS, ROWS, PIX), BF16),
             vmem((BANKS, 2, RIM, PIX), F32),
             vmem((BANKS, 2, RIM, PIX), F32),
             vmem((BANKS, ROWS, PIX + 256), BF16),
@@ -713,8 +764,9 @@
             vmem((2, ROWS, 1024), BF16),
             vmem((ROWS, PIX), F32),
             vmem((BANKS, ROWS, PIX), BF16),
-            dma(11), dma(15), dma(15), dma(15), dma(15), dma(2), dma(2), dma(4), dma(4),
-            dma(4), dma(4), dma(4), dma(4), dma(2), dma(2), dma(4), dma(4), dma(4), dma(4), dma(6), dma(6), dma(2),
+            dma(12), dma(15), dma(15), dma(15), dma(15), dma(2), dma(2), dma(4, 2), dma(4, 2),
+            dma(4, 2), dma(4, 2), dma(4, 2), dma(4, 2), dma(4), dma(4), dma(4, 2), dma(4, 2),
+            dma(4, 2), dma(4, 2), dma(5), dma(5), dma(9),
         ],
         compiler_params=pltpu.CompilerParams(
             collective_id=0, has_side_effects=True, vmem_limit_bytes=60 * 1024 * 1024

time: 81.2 us -> 80.3 us (0.989)
  the two profiles are of different devices: /device:TPU:0 before, /device:TPU:1 now
where the time goes in v3:
time: 80.3 us; the launch traced here: 80.2 us
  Pallas kernels  78.9 us (98%)
  between operations  1.28 us (2%)
    pallas_call x1, Pallas kernels, per_device(): pl.pallas_call(kernel, out_shape=(jax.ShapeDtypeStruct((ROWS, PIX), F32),...  76.5 us
    pallas_call x1, Pallas kernels, per_device(): pl.pallas_call(clip_kernel, out_shape=(jax.ShapeDtypeStruct((ROWS, PIX),...  2.41 us

profile of v3, /device:TPU:1, one launch (start us, length us, event | category | flops | bytes accessed | tf_op | source)
XLA Modules:
  0.0 80.2 jit_solution(17944945254445068838)
XLA Ops:
  1.3 76.5 %shard_map.149 = (f32[128,2048]{1,0:T(8,128)}, bf16[2,128,2048]{2,1,0:T(8,128)(2,1)}) custom-call(f32[128,2048]{1,0:T(8,128)} %bitcast.8, bf16[2,128,2048]{2,1,0:T(8,128)(2,1)} %bitcast.9, s32[1,32]{1,0:T(1,128)} %ids_ref.1, s32[1,1]{1,0:T(1,128)S(6)} %copy.17.counts_ref, bf16[32,32,128]{2,1,0:T(8,128)(2,1)} %bitcast.11, bf16[2,32,32,128]{3,2,1,0:T(8,128)(2,1)} %bitcast.10, ...), custom_call_target="tpu_custom_call" | custom-call | tf_op jit(solution)/shard_map/pallas_call | solution.py:708
  77.7 2.4 %shard_map.150 = (f32[128,2048]{1,0:T(8,128)}, bf16[2,128,2048]{2,1,0:T(8,128)(2,1)}) custom-call(f32[128,2048]{1,0:T(8,128)} %get-tuple-element.6.image_hbm, bf16[2,128,2048]{2,1,0:T(8,128)(2,1)} %get-tuple-element.7.dual_hbm), custom_call_target="tpu_custom_call" | custom-call | tf_op jit(solution)/shard_map/pallas_call | solution.py:783

commit v4 on v3

--- a/solution.py
+++ b/solution.py
@@ -135,10 +135,10 @@
 
 
 def kernel(
-    image_hbm, dual_hbm, ids_ref, counts_ref, weights_hbm, data_hbm,
+    image_hbm, dual_hbm, ids_hbm, counts_hbm, weights_hbm, data_hbm,
     tables_hbm, fourier_hbm, twiddle_hbm, ana_cols_hbm, ana_rows_hbm, syn_rows_hbm, syn_rims_hbm, syn_cols_hbm,
     image_out, dual_out,
-    xpad, xwide, dual, weights, data, tables, fourier, twiddle, ana_cols, ana_rows, syn_rows, syn_rims, syn_cols,
+    ids_ref, counts_ref, xpad, xwide, dual, weights, data, tables, fourier, twiddle, ana_cols, ana_rows, syn_rows, syn_rims, syn_cols,
     basis, folded, ysend, yrecv, hsend, hrecv, coeffs, trial, squares, near, far, quarter_sum, other_sum,
     factor, combined, edge_send, edge_recv, synth_wide, adjoint, own_flat, other_flat, rim_flat,
     w_send, w_recv, d_send, d_recv, ids_send, ids_recv, rim_send, rim_recv, wd_dense,
@@ -158,6 +158,8 @@
     sign = jnp.where(me < 8, 1, -1)
 
     sources = {
+        "ids": (ids_hbm, ids_ref),
+        "counts": (counts_hbm, counts_ref),
         "weights": (weights_hbm, weights),
         "data": (data_hbm, data),
         "image": (image_hbm, xpad.at[RIM : RIM + ROWS]),
@@ -218,6 +220,8 @@
             w_send[rows, :] = dot(picked_rows(weights, i), other_low) + dot(
                 picked_rows(weights, i + 2), other_high
             )
+    loads["ids"].wait()
+    loads["counts"].wait()
     slot = lanes((8, 32))
     ids = jnp.broadcast_to(ids_ref[...], (8, 32))
     live_ids = jnp.where(slot < counts_ref[...], ids, -1).astype(F32).astype(BF16)
@@ -702,7 +706,6 @@
 
 def per_device(constants, image, dual_coeffs, block_ids, block_counts, block_weights, block_data):
     any_space = in_hbm = pl.BlockSpec(memory_space=pl.ANY)
-    in_vmem = pl.BlockSpec(memory_space=pltpu.VMEM)
     dma = lambda *n: pltpu.SemaphoreType.DMA(n)
     vmem = pltpu.VMEM
     image_new, dual_new = pl.pallas_call(
@@ -711,9 +714,11 @@
             jax.ShapeDtypeStruct((ROWS, PIX), F32),
             jax.ShapeDtypeStruct((BANKS, ROWS, PIX), BF16),
         ),
-        in_specs=[any_space, any_space, in_vmem, in_vmem] + [any_space] * 10,
+        in_specs=[any_space] * 4 + [any_space] * 10,
         out_specs=(any_space, any_space),
         scratch_shapes=[
+            vmem((1, 32), jnp.int32),
+            vmem((1, 1), jnp.int32),
             vmem((PAD, PIX), F32),
             vmem((PAD, PIX + 256), BF16),
             vmem((BANKS, ROWS, PIX), BF16),
@@ -764,7 +769,7 @@
             vmem((2, ROWS, 1024), BF16),
             vmem((ROWS, PIX), F32),
             vmem((BANKS, ROWS, PIX), BF16),
-            dma(12), dma(15), dma(15), dma(15), dma(15), dma(2), dma(2), dma(4, 2), dma(4, 2),
+            dma(14), dma(15), dma(15), dma(15), dma(15), dma(2), dma(2), dma(4, 2), dma(4, 2),
             dma(4, 2), dma(4, 2), dma(4, 2), dma(4, 2), dma(4), dma(4), dma(4, 2), dma(4, 2),
             dma(4, 2), dma(4, 2), dma(5), dma(5), dma(9),
         ],

time: 80.3 us -> 79.8 us (level)
  no operation moved by 1% of the time
where the time goes in v4:
time: 79.8 us; the launch traced here: 79.7 us
  Pallas kernels  78.4 us (98%)
  between operations  1.28 us (2%)
    pallas_call x1, Pallas kernels, per_device(): pl.pallas_call(kernel, out_shape=(jax.ShapeDtypeStruct((ROWS, PIX), F32),...  76 us
    pallas_call x1, Pallas kernels, per_device(): pl.pallas_call(clip_kernel, out_shape=(jax.ShapeDtypeStruct((ROWS, PIX),...  2.41 us

profile of v4, /device:TPU:1, one launch (start us, length us, event | category | flops | bytes accessed | tf_op | source)
XLA Modules:
  0.0 79.7 jit_solution(10832191416707424547)
XLA Ops:
  1.3 76.0 %shard_map.149 = (f32[128,2048]{1,0:T(8,128)}, bf16[2,128,2048]{2,1,0:T(8,128)(2,1)}) custom-call(f32[128,2048]{1,0:T(8,128)} %bitcast.8, bf16[2,128,2048]{2,1,0:T(8,128)(2,1)} %bitcast.9, s32[1,32]{1,0:T(1,128)} %ids_hbm.1, s32[1,1]{1,0:T(1,128)S(6)} %copy.17.counts_hbm, bf16[32,32,128]{2,1,0:T(8,128)(2,1)} %bitcast.11, bf16[2,32,32,128]{3,2,1,0:T(8,128)(2,1)} %bitcast.10, ...), custom_call_target="tpu_custom_call" | custom-call | tf_op jit(solution)/shard_map/pallas_call | solution.py:711
  77.3 2.4 %shard_map.150 = (f32[128,2048]{1,0:T(8,128)}, bf16[2,128,2048]{2,1,0:T(8,128)(2,1)}) custom-call(f32[128,2048]{1,0:T(8,128)} %get-tuple-element.6.image_hbm, bf16[2,128,2048]{2,1,0:T(8,128)(2,1)} %get-tuple-element.7.dual_hbm), custom_call_target="tpu_custom_call" | custom-call | tf_op jit(solution)/shard_map/pallas_call | solution.py:788
